TPU v7x, 128 devices: a whole 4x4x4 slice. The times are simulated.
128 devices in a mesh: depth: 4 (over y_lo, core), freq: 32 (over y_hi, z, x).
Axes of the slice: x: 4, y: 4 (y_hi: 2, y_lo: 2; y = y_hi * 2 + y_lo), z: 4, core: 2. Of those that a mesh axis runs over, the one named last changes fastest.
Arguments:
- source_top: bfloat16 [2, 32, 2, 512, 512], P(None, 'freq'), may hold values from -6 to 6
- receiver_top: bfloat16 [2, 32, 2, 512, 512], P(None, 'freq'), may hold values from -6 to 6
- slowness_codes: int32 [4, 1024, 1024], P('depth'), may hold values from 0 to 31
- slowness_table: float32 [32], replicated, may hold values from 0.8 to 1.25
- anchors: int32 [2, 2], replicated, may hold values from 0 to 512, as said below
Outputs:
- image: float32 [4, 15, 512, 512], P('depth', None, 'freq')
Inputs may be any that keep to these rules, and one draw needn't show every extreme that they name: `anchors`: each of the two coordinates is 0 for some shot and 512 for another.
All inputs are finite; a program needn't handle non-finite values.
Results may differ from a plain program's by a relative error of at most 0.03.
Values may be sent and summed in bfloat16 or wider, within the bound.
A program may use at most 192 MiB of HBM per device.

v0:
```python
import math

import jax
import jax.numpy as jnp
from jax import lax
from jax.sharding import PartitionSpec as P

LAG = 7


def shifted_2(block, axis, distance):
    devices = range(lax.axis_size(axis))
    route = [(i - distance, i) for i in devices if i - distance in devices]
    return lax.ppermute(block, axis, route)


def transform_tables(length):
    position = jnp.arange(length, dtype=jnp.int32)
    product = position[:, None] * position[None, :] % length
    angles = product.astype(jnp.float32) * (2.0 * math.pi / length)
    factor = 1.0 / math.sqrt(length)
    return (jnp.cos(angles) * factor, jnp.sin(angles) * factor)


def build_tables(len_x, len_y):
    cos_x, sin_x = transform_tables(len_x)
    cos_y, sin_y = transform_tables(len_y)
    fwd_x = jnp.stack([jnp.stack([cos_x, sin_x]), jnp.stack([-sin_x, cos_x])]).astype(jnp.bfloat16)
    inv_x = jnp.stack([jnp.stack([cos_x, -sin_x]), jnp.stack([sin_x, cos_x])]).astype(jnp.bfloat16)
    fwd_y = jnp.stack(
        [jnp.stack([cos_y, -sin_y], axis=1), jnp.stack([sin_y, cos_y], axis=1)]
    ).astype(jnp.bfloat16)
    inv_y = jnp.stack(
        [jnp.stack([cos_y, sin_y], axis=1), jnp.stack([-sin_y, cos_y], axis=1)]
    ).astype(jnp.bfloat16)
    return (fwd_x, inv_x, fwd_y, inv_y)


def wavenumbers(length):
    position = jnp.arange(length, dtype=jnp.int32)
    signed = jnp.where(position < length // 2, position, position - length)
    return signed.astype(jnp.float32) * (2.0 * math.pi / length)


def aperture_slowness(code_plane, slowness_table, corner, rows_x, rows_y):
    window = lax.dynamic_slice(code_plane, (corner[0], corner[1]), (rows_x, rows_y))
    levels = jnp.arange(slowness_table.shape[0], dtype=jnp.int32)
    return jnp.sum(
        jnp.where(window[None] == levels[:, None, None], slowness_table[:, None, None], 0.0), axis=0
    )


def propagators(slowness, angular, wave_x, wave_y):
    mean_slowness = jnp.mean(slowness)
    vertical = (angular * mean_slowness) ** 2 - wave_x[:, None] ** 2 - wave_y[None, :] ** 2
    travel = jnp.sqrt(jnp.maximum(vertical, 0.0))
    damping = jnp.exp(-jnp.sqrt(jnp.maximum(-vertical, 0.0)))
    screen_angle = angular * (slowness - mean_slowness)
    return (
        damping * jnp.cos(travel),
        damping * jnp.sin(travel),
        jnp.cos(screen_angle),
        jnp.sin(screen_angle),
    )


def advance(fields, tables, operators, kind_signs):
    fwd_x, inv_x, fwd_y, inv_y = tables
    conjugate = kind_signs[None, :, None, None]
    across_x = jnp.einsum(
        "pqxu,gfquy->gfpxy", fwd_x, fields, preferred_element_type=jnp.float32
    ).astype(jnp.bfloat16)
    second = jnp.einsum("gfqxu,qupb->gfxpb", across_x, fwd_y, preferred_element_type=jnp.float32)
    real_part = second[:, :, :, 0]
    imag_part = second[:, :, :, 1]
    phase_re = operators[0][:, None]
    phase_im = operators[1][:, None] * conjugate
    shifted = jnp.stack(
        [real_part * phase_re - imag_part * phase_im, real_part * phase_im + imag_part * phase_re],
        axis=3,
    ).astype(jnp.bfloat16)
    back_y = jnp.einsum(
        "gfxqu,qupb->gfxpb", shifted, inv_y, preferred_element_type=jnp.float32
    ).astype(jnp.bfloat16)
    fourth = jnp.einsum("pqxu,gfuqy->gfpxy", inv_x, back_y, preferred_element_type=jnp.float32)
    real_part = fourth[:, :, 0]
    imag_part = fourth[:, :, 1]
    turn_re = operators[2][:, None]
    turn_im = operators[3][:, None] * conjugate
    return jnp.stack(
        [real_part * turn_re - imag_part * turn_im, real_part * turn_im + imag_part * turn_re],
        axis=2,
    ).astype(jnp.bfloat16)


def correlate(source, receiver, row_count):
    lag_terms = []
    for offset in range(-LAG, LAG + 1):
        shifted_source = source[:, :, :, LAG - offset : LAG - offset + row_count].astype(
            jnp.float32
        )
        shifted_receiver = receiver[:, :, :, LAG + offset : LAG + offset + row_count].astype(
            jnp.float32
        )
        lag_terms.append(jnp.sum(shifted_source * shifted_receiver, axis=(1, 2)))
    return jnp.stack(lag_terms, axis=1)


def keep_all(carried):
    return carried


def shards(source_top, receiver_top, slowness_codes, slowness_table, anchors):
    shot_count, freq_dev, unused_parts, rows_x, rows_y = source_top.shape
    planes = slowness_codes.shape[0]
    freq_count = lax.axis_size("freq")
    depth_count = lax.axis_size("depth")
    freq_total = freq_count * freq_dev
    depth_index = lax.axis_index("depth")
    factor = 1.0 / math.sqrt(2.0 * shot_count * freq_total)
    tables = build_tables(rows_x, rows_y)
    wave_x = wavenumbers(rows_x)
    wave_y = wavenumbers(rows_y)
    freq_first = lax.axis_index("freq") * freq_dev
    positions = (freq_first + jnp.arange(freq_dev, dtype=jnp.int32)).astype(jnp.float32)
    angular = jnp.reshape(math.pi * (0.45 + 0.5 * (positions + 0.5) / freq_total), (freq_dev, 1, 1))
    top_fields = jnp.stack([source_top, receiver_top], axis=2)
    both_signs = jnp.array([1.0, -1.0], jnp.float32)

    def descend(current, shot_index):
        corner = anchors[shot_index]
        slowness = aperture_slowness(slowness_codes[0], slowness_table, corner, rows_x, rows_y)
        operators = propagators(slowness, angular, wave_x, wave_y)
        current = advance(current, tables, operators, both_signs)
        plane_fields = [current]
        return (current, jnp.stack(plane_fields))

    def record_shot(record, plane_stack):
        padded = jnp.pad(plane_stack, ((0, 0), (0, 0), (0, 0), (0, 0), (LAG, LAG), (0, 0)))
        return record + correlate(padded[:, :, 0], padded[:, :, 1], rows_x)

    record = jnp.zeros((planes, 2 * LAG + 1, rows_x, rows_y), jnp.float32)

    def run_all(carried):

        def per_shot(shot_index, inner_carry):
            states, record_now = inner_carry
            new_state, plane_stack = descend(states[shot_index], shot_index)
            states = lax.dynamic_update_index_in_dim(states, new_state, shot_index, 0)
            return (states, record_shot(record_now, plane_stack))

        return lax.fori_loop(0, shot_count, per_shot, carried)

    def segment_all(segment_index, carried):
        return lax.cond(depth_index == segment_index, run_all, keep_all, carried)

    def later_all(segment_index, carried):
        incoming, record_now = carried
        incoming = shifted_2(incoming, "depth", 1)
        return segment_all(segment_index, (incoming, record_now))

    carried = segment_all(0, (top_fields, record))
    unused_fields, record = lax.fori_loop(1, depth_count, later_all, carried)
    return lax.psum_scatter(
        (record * factor).astype(jnp.bfloat16), "freq", scatter_dimension=2, tiled=True
    ).astype(jnp.float32)


def solution(mesh):
    return jax.shard_map(
        shards,
        mesh=mesh,
        in_specs=(
            P(None, "freq", None, None, None),
            P(None, "freq", None, None, None),
            P("depth", None, None),
            P(),
            P(),
        ),
        out_specs=P("depth", None, "freq", None),
        check_vma=False,
    )
```

profile of v0, /device:TPU:8, one launch (start us, length us, event | category | flops | bytes accessed | tf_op | source)
XLA Modules:
  0.0 1151.3 jit_solution(18234246018306094963)
XLA Ops:
  6.5 4.0 multiply_convert_fusion.2
  10.5 4.0 negate_convert_fusion.1
  14.5 4.6 fusion.115
  19.2 4.6 multiply_convert_fusion.1
  23.8 4.6 fusion.116
  28.4 4.6 negate_convert_fusion
  35.4 4.3 copy.83
  51.6 8.5 conditional.2
  51.6 7.5 broadcast_in_dim.145
  60.2 709.2 %while.56 = (s32[]{:T(128)}, bf16[2,1,2,2,512,512]{4,5,3,2,1,0:T(8,128)(2,1)}, f32[1,15,512,512]{3,2,1,0:T(8,128)}, s32[]{:T(128)}, bf16[2,2,512,512]{3,2,1,0:T(...) while((s32[]{:T(128)}, ...), condition=%wide.region_43.44_spmd.clone.clone.clone, body=%wide.region_21.43_spmd.sunk.clone.clone.clone.sunk | while | flops 8671726592 | bytes 265363184 | solution.py:163
  63.2 48.2 %collective-permute-done = bf16[2,1,2,2,512,512]{4,5,3,2,1,0:T(8,128)(2,1)} collective-permute-done((bf16[2,1,2,2,512,512]{4,5,3,2,1,0:T(8,128)(2,1)}, bf16[2,1,2,2,512,512]{4,5,3,2,1,0:T(8,128)(2,1)}, u32[]{:S(2)}, u32[]{:S(2)}) %collective-permute-start) | collective-permute-done | bytes 4194336 | tf_op jit(solution)/shard_map/while/body/eval_jaxpr/ppermute | solution.py:14
  112.6 4.4 copy.196
  119.0 391.0 %collective-permute-done = bf16[2,1,2,2,512,512]{4,5,3,2,1,0:T(8,128)(2,1)} collective-permute-done((bf16[2,1,2,2,512,512]{4,5,3,2,1,0:T(8,128)(2,1)}, bf16[2,1,2,2,512,512]{4,5,3,2,1,0:T(8,128)(2,1)}, u32[]{:S(2)}, u32[]{:S(2)}) %collective-permute-start) | collective-permute-done | bytes 4194336 | tf_op jit(solution)/shard_map/while/body/eval_jaxpr/ppermute | solution.py:14
  509.9 197.5 %conditional.8 = ((bf16[2,1,2,2,512,512]{4,5,3,2,1,0:T(8,128)(2,1)}, f32[1,15,512,512]{3,2,1,0:T(8,128)})) conditional(s32[]{:T(128)} %convert_element_type.981, (bf16[2,1,2,2,512,512]{4,5,3,2,1,0:T(8,128)(2,1)}, f32[1,15,512,512]{3,2,1,0:T(8,128)}) %tuple.207, (f32[512]{0:T(512)S(1)}, bf16[2,2,512,512]{3,2,1,0:T(8,128)(2,1)}, ...), branch_computations={%region_22.22_spmd, %region_23.42_spmd.clone} | conditional | flops 8671724544 | bytes 240195008 | solution.py:155
  510.0 196.3 %while.54 = (s32[]{:T(128)}, bf16[2,1,2,2,512,512]{4,5,3,2,1,0:T(8,128)(2,1)}, f32[1,15,512,512]{3,2,1,0:T(8,128)}, bf16[2,2,512,512]{3,2,1,0:T(8,128)(2,1)}, bf...) while((s32[]{:T(128)}, ...), condition=%wide.region_42.41_spmd, body=%wide.region_24.40_spmd.sunk | while | flops 8671723520 | bytes 240190720 | solution.py:152
  510.0 9.3 convolution_bitcast_fusion.8
  525.2 14.8 %select_reduce_fusion.6 = (f32[512,512]{1,0:T(8,128)S(1)}, f32[]{:T(128)}) fusion(f32[32]{0:T(128)S(1)} %copy-done.18, s32[512,512]{1,0:T(8,128)S(1)} %dynamic-slice_bitcast_fusion.4), kind=kLoop, calls=%fused_computation.1.clone.1 | loop fusion | flops 33292288 | bytes 2097284 | tf_op jit(solution)/shard_map/while/body/eval_jaxpr/cond/branch_1_fun/while/body/eval_jaxpr/reduce_sum | solution.py:48
  540.6 4.4 fusion.163
  555.2 3.8 fusion.166
  576.8 5.1 multiply_reduce_fusion.35
  591.5 16.0 %add.354 = f32[1,15,512,512]{3,2,1,0:T(8,128)} add(f32[1,15,512,512]{3,2,1,0:T(8,128)} %get-tuple-element.1827, f32[1,15,512,512]{3,2,1,0:T(8,128)} %bitcast_dynamic-update-slice_fusion.74) | non-fusion elementwise | flops 3932160 | bytes 47185920 | tf_op jit(solution)/shard_map/while/body/eval_jaxpr/cond/branch_1_fun/while/body/eval_jaxpr/add | solution.py:140
  607.6 9.3 convolution_bitcast_fusion.8
  622.9 15.0 %select_reduce_fusion.6 = (f32[512,512]{1,0:T(8,128)S(1)}, f32[]{:T(128)}) fusion(f32[32]{0:T(128)S(1)} %copy-done.18, s32[512,512]{1,0:T(8,128)S(1)} %dynamic-slice_bitcast_fusion.4), kind=kLoop, calls=%fused_computation.1.clone.1 | loop fusion | flops 33292288 | bytes 2097284 | tf_op jit(solution)/shard_map/while/body/eval_jaxpr/cond/branch_1_fun/while/body/eval_jaxpr/reduce_sum | solution.py:48
  638.5 4.4 fusion.163
  652.9 3.8 fusion.166
  674.5 5.1 multiply_reduce_fusion.35
  689.1 16.0 %add.354 = f32[1,15,512,512]{3,2,1,0:T(8,128)} add(f32[1,15,512,512]{3,2,1,0:T(8,128)} %get-tuple-element.1827, f32[1,15,512,512]{3,2,1,0:T(8,128)} %bitcast_dynamic-update-slice_fusion.74) | non-fusion elementwise | flops 3932160 | bytes 47185920 | tf_op jit(solution)/shard_map/while/body/eval_jaxpr/cond/branch_1_fun/while/body/eval_jaxpr/add | solution.py:140
  707.4 4.4 copy.196
  714.0 48.2 %collective-permute-done = bf16[2,1,2,2,512,512]{4,5,3,2,1,0:T(8,128)(2,1)} collective-permute-done((bf16[2,1,2,2,512,512]{4,5,3,2,1,0:T(8,128)(2,1)}, bf16[2,1,2,2,512,512]{4,5,3,2,1,0:T(8,128)(2,1)}, u32[]{:S(2)}, u32[]{:S(2)}) %collective-permute-start) | collective-permute-done | bytes 4194336 | tf_op jit(solution)/shard_map/while/body/eval_jaxpr/ppermute | solution.py:14
  762.4 4.4 copy.196
  769.4 10.9 multiply_convert_fusion
  780.3 362.0 %reduce-scatter.2.cloned.1.call-done = bf16[1,15,16,512]{3,2,1,0:T(8,128)(2,1)} async-done(((bf16[1,15,512,512]{3,2,1,0:T(8,128)(2,1)}), bf16[1,15,16,512]{3,2,1,0:T(8,128)(2,1)}) %reduce-scatter.2.cloned.1.call-update) | async-done | bytes 245776 | tf_op jit(solution)/shard_map/reduce_scatter | solution.py:164
  (119 shorter events, 102.5 us)
Async XLA Ops:
  6.5 26.5 %copy-start.7 = (bf16[2,1,2,512,512]{4,3,2,1,0:T(8,128)(2,1)S(1)}, bf16[2,1,2,512,512]{4,3,2,1,0:T(8,128)(2,1)}, u32[]{:S(2)}) copy-start(bf16[2,1,2,512,512]{4,3,2,1,0:T(8,128)(2,1)} %param.17) | copy-start | bytes 6291460
  6.5 1135.8 %reduce-scatter.2.cloned.1.call-start = ((), (), s32[]{:S(2)}) async-start(), calls=%async_computation.1 | async-start | bytes 8110080 | tf_op jit(solution)/shard_map/reduce_scatter | solution.py:164
  35.4 4.3 copy-start.14
  35.4 4.3 copy-start.15
  35.4 4.3 copy-start.16
  40.4 2.0 copy-start.2
  42.3 2.3 copy-start.4
  42.4 3.0 copy-start.5
  61.3 50.1 %collective-permute-start = (bf16[2,1,2,2,512,512]{4,5,3,2,1,0:T(8,128)(2,1)}, bf16[2,1,2,2,512,512]{4,5,3,2,1,0:T(8,128)(2,1)}, u32[]{:S(2)}, u32[]{:S(2)}) collective-permute-start(bf16[2,1,2,2,512,512]{4,5,3,2,1,0:T(8,128)(2,1)} %get-tuple-element.1937), channel_id=1, source_target_pairs={{0,32},{32,64},{64,96},{1,33},{33,65},{65,97},{2,34},{34,66},{66,9... | collective-permute-start | bytes 12582920 | tf_op jit(solution)/shard_map/while/body/eval_jaxpr/ppermute | solution.py:14
  117.1 392.9 %collective-permute-start = (bf16[2,1,2,2,512,512]{4,5,3,2,1,0:T(8,128)(2,1)}, bf16[2,1,2,2,512,512]{4,5,3,2,1,0:T(8,128)(2,1)}, u32[]{:S(2)}, u32[]{:S(2)}) collective-permute-start(bf16[2,1,2,2,512,512]{4,5,3,2,1,0:T(8,128)(2,1)} %get-tuple-element.1937), channel_id=1, source_target_pairs={{0,32},{32,64},{64,96},{1,33},{33,65},{65,97},{2,34},{34,66},{66,9... | collective-permute-start | bytes 12582920 | tf_op jit(solution)/shard_map/while/body/eval_jaxpr/ppermute | solution.py:14
  510.0 9.3 copy-start.21
  519.3 5.8 copy-start.18
  525.1 19.8 %copy-start.6 = (f32[2]{0:T(128)S(1)}, f32[2]{0:T(128)}, u32[]{:S(2)}) copy-start(f32[2]{0:T(128)} %get-tuple-element.1854) | copy-start | bytes 28 | tf_op jit(solution)/shard_map/while/body/eval_jaxpr/cond/branch_1_fun/while
  545.0 3.5 copy-start
  548.4 1.6 copy-start.8
  550.0 2.3 copy-start.13
  607.6 9.3 copy-start.21
  616.9 5.9 copy-start.18
  622.9 20.1 %copy-start.6 = (f32[2]{0:T(128)S(1)}, f32[2]{0:T(128)}, u32[]{:S(2)}) copy-start(f32[2]{0:T(128)} %get-tuple-element.1854) | copy-start | bytes 28 | tf_op jit(solution)/shard_map/while/body/eval_jaxpr/cond/branch_1_fun/while
  642.9 3.5 copy-start
  646.4 1.6 copy-start.8
  648.0 2.3 copy-start.13
  712.1 50.1 %collective-permute-start = (bf16[2,1,2,2,512,512]{4,5,3,2,1,0:T(8,128)(2,1)}, bf16[2,1,2,2,512,512]{4,5,3,2,1,0:T(8,128)(2,1)}, u32[]{:S(2)}, u32[]{:S(2)}) collective-permute-start(bf16[2,1,2,2,512,512]{4,5,3,2,1,0:T(8,128)(2,1)} %get-tuple-element.1937), channel_id=1, source_target_pairs={{0,32},{32,64},{64,96},{1,33},{33,65},{65,97},{2,34},{34,66},{66,9... | collective-permute-start | bytes 12582920 | tf_op jit(solution)/shard_map/while/body/eval_jaxpr/ppermute | solution.py:14
Sparse Core Ops, SparseCore 0:
  780.5 361.8 reduce-scatter.1
where the time goes:
time: 1160 us; the launch traced here: 1150 us
  waiting for transfers between devices  849 us (73%)
  other arithmetic  154 us (13%)
  local copies, waits for them, and re-layouts  82.6 us (7%)
  matrix products  28.6 us (2%)
  loops' own time  17.6 us (2%)
  between operations  13.8 us (1%)
    ppermute x3, waiting for transfers between devices, shifted_2(): return lax.ppermute(block, axis, route)  487 us
    reduce_scatter x1, waiting for transfers between devices, shards(): lax.psum_scatter((record * factor).astype(jnp.bfloat16), 'freq', scatter_...  362 us
    while x55, local copies, waits for them, and re-layouts  45 us
    add x2, other arithmetic, record_shot(): return record + correlate(padded[:, :, 0], padded[:, :, 1], rows_x)  31.9 us
    reduce_sum x2, other arithmetic, aperture_slowness(): jnp.sum(jnp.where(window[None] == levels[:, None, None], slowness_table[:...  29.8 us
    another operation x6, other arithmetic  26.5 us
  transfers between devices with their start and end apart: 4, of which 4 were waited for; matrix products, arithmetic and copies ran while one was open for 0% of the time, Pallas kernels for 0%

commit v1 on v0

v1 whole, which is shorter than its diff:
```python
import functools
import math

import jax
import jax.numpy as jnp
import numpy as np
from jax import lax
from jax.experimental import pallas as pl
from jax.experimental.pallas import tpu as pltpu
from jax.sharding import PartitionSpec as P

LAG = 7
LAGS = 2 * LAG + 1
N = 512
B = 128
GROUPS = 5
PER = LAGS // GROUPS
MESH = pl.DeviceIdType.MESH
F32 = jnp.float32
BF16 = jnp.bfloat16


def butterfly_matrices():
    j = np.arange(B)[:, None]
    k = np.arange(B)[None, :]
    mats = []
    for wave in (4 * k, 4 * k + 1, 4 * k + 2, -(4 * k + 1)):
        angle = 2.0 * np.pi * ((j * wave) % N) / N
        c = np.cos(angle) / math.sqrt(N)
        s = np.sin(angle) / math.sqrt(N)
        mats.append(np.block([[c, -s], [s, c]]))
    right = np.stack(mats)
    return right, np.swapaxes(right, 1, 2)


def even_poly(first, terms, top, samples=400):
    q = (np.cos(np.pi * (np.arange(samples) + 0.5) / samples) + 1.0) * 0.5 * top
    r = np.sqrt(q)
    want = np.cos(r) if first == 0 else np.sin(r) / r
    fit = np.polynomial.Chebyshev.fit(q, want, terms, domain=[0, top])
    return [float(v) for v in fit.convert(kind=np.polynomial.Polynomial).coef]


COS_Q = even_poly(0, 9, 14.0)
SIN_Q = even_poly(1, 9, 14.0)


def horner(coefs, q):
    value = coefs[-1] * q + coefs[-2]
    for c in coefs[-3::-1]:
        value = value * q + c
    return value


def split4(re, im):
    er, ei, dr, di = re[0] + re[2], im[0] + im[2], re[0] - re[2], im[0] - im[2]
    fr, fi, gr, gi = re[1] + re[3], im[1] + im[3], re[1] - re[3], im[1] - im[3]
    return (er + fr, dr + gi, er - fr, dr - gi), (ei + fi, di - gr, ei - fi, di + gr)


def join4(re, im):
    er, ei, dr, di = re[0] + re[2], im[0] + im[2], re[0] - re[2], im[0] - im[2]
    fr, fi, gr, gi = re[1] + re[3], im[1] + im[3], re[1] - re[3], im[1] - im[3]
    return (er + fr, dr - gi, er - fr, dr + gi), (ei + fi, di + gr, ei - fi, di - gr)


def fields_kernel(
    src, rec, codes, table, right_ref, left_ref, out,
    u, a, cbuf, ph, sc, tsem, csem, osem,
):
    depth = lax.axis_index("depth")
    core = depth % 2
    first_plane = (depth // 2) * 2
    steps = first_plane + 2
    position = lax.axis_index("freq").astype(F32)
    angular = math.pi * (0.45 + 0.5 * (position + 0.5) / 32.0)

    tops = []
    for kind, top in enumerate((src, rec)):
        for q in range(4):
            tops.append(pltpu.make_async_copy(
                top.at[core, 0, :, :, pl.ds(q * B, B)], u.at[kind, :, q], tsem.at[kind, q]))
    for copy in tops:
        copy.start()
    for z in range(4):
        pltpu.make_async_copy(codes.at[z, core], cbuf.at[z], csem.at[z]).start()

    lane = lax.broadcasted_iota(jnp.int32, (8, B), 1)
    levels = jnp.zeros((8, B), F32)
    for k in range(32):
        levels = jnp.where(lane == k, table[k], levels)

    def lookup(values, index):
        return jnp.take_along_axis(jnp.tile(values, (index.shape[0] // 8, 1)), index, axis=1)

    for copy in tops:
        copy.wait()

    def step(z, carry):
        pltpu.make_async_copy(codes.at[z, core], cbuf.at[z], csem.at[z]).wait()

        def add_rows(i, total):
            for q in range(4):
                index = cbuf[z, pl.ds(i * 32, 32), q * B:(q + 1) * B].astype(jnp.int32)
                got = lookup(levels, index)
                total = total + (got[0:8] + got[8:16]) + (got[16:24] + got[24:32])
            return total

        total = lax.fori_loop(0, N // 32, add_rows, jnp.zeros((8, B), F32))
        base = jnp.sum(total) * (1.0 / (N * N))

        def phase_block(n, carry):
            rx, ry = n // 3, n % 3
            kx = lax.broadcasted_iota(jnp.int32, (B, B), 0) * 4 + rx
            ky = lax.broadcasted_iota(jnp.int32, (B, B), 1) * 4 + ry
            kx = jnp.where(kx < N // 2, kx, kx - N).astype(F32) * (2.0 * math.pi / N)
            ky = jnp.where(ky < N // 2, ky, ky - N).astype(F32) * (2.0 * math.pi / N)
            q = (angular * base) ** 2 - kx * kx - ky * ky
            root = jnp.sqrt(jnp.abs(q))
            decay = jnp.exp(-root)
            wave = jnp.maximum(q, 0.0)
            ph[0, rx, ry] = jnp.where(q >= 0.0, horner(COS_Q, wave), decay)
            ph[1, rx, ry] = jnp.where(q >= 0.0, root * horner(SIN_Q, wave), 0.0)
            return carry

        lax.fori_loop(0, 9, phase_block, 0)

        angle = angular * (levels - base)
        squared = angle * angle
        cos_levels = horner(COS_Q, squared)
        sin_levels = angle * horner(SIN_Q, squared)

        def screen_rows(i, carry):
            rows = pl.ds(i * 32, 32)
            for q in range(4):
                index = cbuf[z, rows, q * B:(q + 1) * B].astype(jnp.int32)
                sc[0, q, rows, :] = lookup(cos_levels, index)
                sc[1, q, rows, :] = lookup(sin_levels, index)
            return carry

        lax.fori_loop(0, N // 32, screen_rows, 0)

        def wide(ref, kind, p, half, block):
            rows = slice(block * B, (block + 1) * B)
            return jnp.concatenate([ref[kind, p, half * 2, rows, :], ref[kind, p, half * 2 + 1, rows, :]], axis=1)

        def put_wide(ref, kind, p, half, block, value):
            rows = slice(block * B, (block + 1) * B)
            ref[kind, p, half * 2, rows, :] = value[:, :B]
            ref[kind, p, half * 2 + 1, rows, :] = value[:, B:]

        def forward_x(n, carry):
            kind, half = n // 2, n % 2
            re = [wide(u, kind, 0, half, q) for q in range(4)]
            im = [wide(u, kind, 1, half, q) for q in range(4)]
            sre, sim = split4(re, im)
            for r in range(4):
                got = jnp.dot(left_ref[r], jnp.concatenate([sre[r], sim[r]], axis=0),
                              preferred_element_type=F32).astype(BF16)
                put_wide(a, kind, 0, half, r, got[:B])
                put_wide(a, kind, 1, half, r, got[B:])
            return carry

        lax.fori_loop(0, 4, forward_x, 0)

        def along_y(n, carry):
            kind, rx = n // 4, n % 4
            sign = (1 - 2 * kind).astype(F32)
            px = jnp.where(rx == 3, 1, rx)
            rows = pl.ds(pl.multiple_of(rx * B, B), B)
            re = [a[kind, 0, q, rows, :] for q in range(4)]
            im = [a[kind, 1, q, rows, :] for q in range(4)]
            sre, sim = split4(re, im)
            tre, tim = [], []
            for r in range(4):
                got = jnp.dot(jnp.concatenate([sre[r], sim[r]], axis=1), right_ref[r],
                              preferred_element_type=F32)
                gre, gim = got[:, :B], got[:, B:]
                py = 1 if r == 3 else r
                pre, pim = ph[0, px, py], ph[1, px, py] * sign
                turned = jnp.concatenate(
                    [(gre * pre - gim * pim).astype(BF16), (gre * pim + gim * pre).astype(BF16)], axis=1)
                back = jnp.dot(turned, left_ref[r], preferred_element_type=F32)
                tre.append(back[:, :B])
                tim.append(back[:, B:])
            cre, cim = join4(tre, tim)
            for q in range(4):
                a[kind, 0, q, rows, :] = cre[q].astype(BF16)
                a[kind, 1, q, rows, :] = cim[q].astype(BF16)
            return carry

        lax.fori_loop(0, 8, along_y, 0)

        @pl.when(z > first_plane)
        def _():
            pltpu.make_async_copy(u, out.at[0], osem.at[0]).wait()

        def inverse_x(n, carry):
            kind, half = n // 2, n % 2
            sign = (1 - 2 * kind).astype(F32)
            tre, tim = [], []
            for r in range(4):
                data = jnp.concatenate([wide(a, kind, 0, half, r), wide(a, kind, 1, half, r)], axis=0)
                got = jnp.dot(right_ref[r], data, preferred_element_type=F32)
                tre.append(got[:B])
                tim.append(got[B:])
            xre, xim = join4(tre, tim)
            for q in range(4):
                rows = slice(q * B, (q + 1) * B)
                for part in range(2):
                    cols = slice(part * B, (part + 1) * B)
                    cre = sc[0, half * 2 + part, rows, :]
                    cim = sc[1, half * 2 + part, rows, :] * sign
                    gre, gim = xre[q][:, cols], xim[q][:, cols]
                    u[kind, 0, half * 2 + part, rows, :] = (gre * cre - gim * cim).astype(BF16)
                    u[kind, 1, half * 2 + part, rows, :] = (gre * cim + gim * cre).astype(BF16)
            return carry

        lax.fori_loop(0, 4, inverse_x, 0)

        @pl.when(z == first_plane)
        def _():
            pltpu.make_async_copy(u, out.at[0], osem.at[0]).start()

        @pl.when(z == first_plane + 1)
        def _():
            pltpu.make_async_copy(u, out.at[1], osem.at[1]).start()

        return carry

    lax.fori_loop(0, steps, step, 0)

    def drain(z, carry):
        pltpu.make_async_copy(codes.at[z, core], cbuf.at[z], csem.at[z]).wait()
        return carry

    lax.fori_loop(steps, 4, drain, 0)
    pltpu.make_async_copy(u, out.at[1], osem.at[1]).wait()


def make_fields(src, rec, codes, table, right, left):
    vmem = pl.BlockSpec(memory_space=pltpu.VMEM)
    hbm = pl.BlockSpec(memory_space=pl.ANY)
    return pl.pallas_call(
        fields_kernel,
        out_shape=jax.ShapeDtypeStruct((2, 2, 2, 4, N, B), BF16),
        in_specs=[hbm, hbm, hbm, pl.BlockSpec(memory_space=pltpu.SMEM), vmem, vmem],
        out_specs=hbm,
        scratch_shapes=[
            pltpu.VMEM((2, 2, 4, N, B), BF16),
            pltpu.VMEM((2, 2, 4, N, B), BF16),
            pltpu.VMEM((4, N, N), BF16),
            pltpu.VMEM((2, 3, 3, B, B), F32),
            pltpu.VMEM((2, 4, N, B), F32),
            pltpu.SemaphoreType.DMA((2, 4)),
            pltpu.SemaphoreType.DMA((4,)),
            pltpu.SemaphoreType.DMA((2,)),
        ],
        compiler_params=pltpu.CompilerParams(vmem_limit_bytes=60 * 1024 * 1024),
        name="fields",
    )(src, rec, codes, table, right, left)


def image_kernel(factor, fields, out, own, other, pad, buf, r0, r1, r2, r3, r4,
                 lsem, ssem, rsem, xs, xr):
    depth = lax.axis_index("depth")
    freq = lax.axis_index("freq")
    core = depth % 2
    x, z, yh = freq % 4, (freq // 4) % 4, freq // 16
    base = yh * 16 + z * 4 + x
    sibling = (depth + 1 - 2 * core, freq)
    dims = (
        (depth, base - x + (x + 1 - 2 * (x % 2))),
        (depth, base - x + (3 - x)),
        (depth, base - 4 * z + 4 * (z + 1 - 2 * (z % 2))),
        (depth, base - 4 * z + 4 * (3 - z)),
    )
    across = (depth, base - 16 * yh + 16 * (1 - yh))

    barrier = pltpu.get_barrier_semaphore()
    for who in (sibling, across) + dims:
        pl.semaphore_signal(barrier, inc=1, device_id=who, device_id_type=MESH)
    local = pltpu.make_async_copy(fields.at[core], own, lsem)
    local.start()
    pl.semaphore_wait(barrier, 6)
    swap = pltpu.make_async_remote_copy(
        src_ref=fields.at[1 - core], dst_ref=other, send_sem=xs, recv_sem=xr,
        device_id=sibling, device_id_type=MESH)
    swap.start()

    for s in range(2):
        for k in range(2):
            for p in range(2):
                for i in range(4):
                    pad[s, k, p, i, 0:8, :] = jnp.zeros((8, B), F32)
                    pad[s, k, p, i, N + 8:N + 16, :] = jnp.zeros((8, B), F32)

    def widen(s, ref):
        def body(n, carry):
            k, p, i = n // 8, (n // 4) % 2, n % 4
            for h in range(2):
                pad[s, k, p, i, 8 + h * 256:8 + (h + 1) * 256, :] = ref[k, p, i, h * 256:(h + 1) * 256, :].astype(F32)
            return carry
        lax.fori_loop(0, 16, body, 0)

    local.wait()
    widen(0, own)
    swap.wait()
    widen(1, other)

    def bits(ix, iz):
        return [((ix + 1) // 2) % 2, ix // 2, ((iz + 1) // 2) % 2, iz // 2]

    mine = bits(x, z)

    def produce(g):
        def body(n, carry):
            i, f = n // 32, n % 32
            theirs = bits(f % 4, (f // 4) % 4)
            rel = [(m + t) % 2 for m, t in zip(mine, theirs)]
            ybit = (yh + f // 16) % 2
            slot = ybit
            for t in range(4):
                d = (i + t) % 4
                pick = jnp.where(d == 0, rel[0], jnp.where(d == 1, rel[1], jnp.where(d == 2, rel[2], rel[3])))
                slot = slot + pick * (16 >> t)
            row = f * 16
            for l in range(PER):
                h = g * PER + l - LAG
                total = None
                for s in range(2):
                    for p in range(2):
                        left = pad[s, 0, p, i, pl.ds(row + (8 - h), 16), :]
                        right = pad[s, 1, p, i, pl.ds(row + (8 + h), 16), :]
                        term = left * right
                        total = term if total is None else total + term
                buf[g, i, slot, l] = total.astype(BF16)
            return carry
        lax.fori_loop(0, 128, body, 0)

    recv = (r0, r1, r2, r3, r4)

    def copy(g, i, t):
        half = 16 >> t
        who = across if t == 4 else dims[(i + t) % 4]
        return pltpu.make_async_remote_copy(
            src_ref=buf.at[g, i, pl.ds(half, half)], dst_ref=recv[t].at[g, i],
            send_sem=ssem.at[g, i, t], recv_sem=rsem.at[g, i, t],
            device_id=who, device_id_type=MESH)

    def arrive(g, i, t):
        copy(g, i, t).wait_recv()
        half = 16 >> t

        if t < 4:
            def body(n, carry):
                k = half - 1 - n
                buf[g, i, k] = buf[g, i, k] + recv[t][g, i, k]
                return carry
            lax.fori_loop(0, half, body, 0)
            copy(g, i, t + 1).start()
        else:
            total = buf[g, i, 0].astype(F32) + recv[4][g, i, 0].astype(F32)
            out[g * PER:(g + 1) * PER, :, i * B:(i + 1) * B] = total * factor

    for g in range(GROUPS):
        produce(g)
        for i in range(4):
            copy(g, i, 0).start()
    for w in range(GROUPS + 4):
        for t in range(4, -1, -1):
            g = w - t
            if 0 <= g < GROUPS:
                for i in range(4):
                    arrive(g, i, t)
    for g in range(GROUPS):
        for i in range(4):
            for t in range(5):
                copy(g, i, t).wait_send()


def make_image(fields, factor):
    hbm = pl.BlockSpec(memory_space=pl.ANY)
    strip = (PER, 16, B)
    return pl.pallas_call(
        functools.partial(image_kernel, factor),
        out_shape=jax.ShapeDtypeStruct((LAGS, 16, N), F32),
        in_specs=[hbm],
        out_specs=pl.BlockSpec(memory_space=pltpu.VMEM),
        scratch_shapes=[
            pltpu.VMEM((2, 2, 4, N, B), BF16),
            pltpu.VMEM((2, 2, 4, N, B), BF16),
            pltpu.VMEM((2, 2, 2, 4, N + 16, B), F32),
            pltpu.VMEM((GROUPS, 4, 32) + strip, BF16),
            pltpu.VMEM((GROUPS, 4, 16) + strip, BF16),
            pltpu.VMEM((GROUPS, 4, 8) + strip, BF16),
            pltpu.VMEM((GROUPS, 4, 4) + strip, BF16),
            pltpu.VMEM((GROUPS, 4, 2) + strip, BF16),
            pltpu.VMEM((GROUPS, 4, 1) + strip, BF16),
            pltpu.SemaphoreType.DMA,
            pltpu.SemaphoreType.DMA((GROUPS, 4, 5)),
            pltpu.SemaphoreType.DMA((GROUPS, 4, 5)),
            pltpu.SemaphoreType.DMA,
            pltpu.SemaphoreType.DMA,
        ],
        compiler_params=pltpu.CompilerParams(
            collective_id=1, has_side_effects=True, vmem_limit_bytes=60 * 1024 * 1024),
        name="image",
    )(fields)


def shards(source_top, receiver_top, slowness_codes, slowness_table, anchors):
    right, left = butterfly_matrices()
    right = jnp.asarray(right, BF16)
    left = jnp.asarray(left, BF16)
    windows = jnp.stack([
        lax.dynamic_slice(slowness_codes[0], (anchors[s, 0], anchors[s, 1]), (N, N)) for s in range(2)
    ]).astype(BF16)
    windows = lax.all_gather(windows, "depth")
    fields = make_fields(source_top, receiver_top, windows, slowness_table, right, left)
    image = make_image(fields, 1.0 / math.sqrt(128.0))
    return image[None]


def solution(mesh):
    return jax.shard_map(
        shards,
        mesh=mesh,
        in_specs=(
            P(None, "freq", None, None, None),
            P(None, "freq", None, None, None),
            P("depth", None, None),
            P(),
            P(),
        ),
        out_specs=P("depth", None, "freq", None),
        check_vma=False,
    )
```

time: 1160 us -> 239 us (0.21)
  waiting for transfers between devices: 849 us -> 47.3 us
  Pallas kernels: 0 us -> 164 us
  other arithmetic: 154 us -> 3.33 us
  local copies, waits for them, and re-layouts: 82.6 us -> 3.28 us
  matrix products: 28.6 us -> 0 us
  loops' own time: 17.6 us -> 0 us
    ppermute x3 -> x0, waiting for transfers between devices: 487 us -> none  [shifted_2(): return lax.ppermute(block, axis, route)]
    reduce_scatter x1 -> x0, waiting for transfers between devices: 362 us -> none  [shards(): lax.psum_scatter((record * factor).astype(jnp.bfloat16), 'freq', scatter_...]
    pallas_call x0 -> x2, Pallas kernels: none -> 164 us  [the longest x1 110 us: make_image(): pl.pallas_call(functools.partial(image_kernel, factor), out_shape=jax.Sha...]
    all_gather x0 -> x1, waiting for transfers between devices: none -> 47.2 us  [shards(): windows = lax.all_gather(windows, 'depth')]
    reduce_sum x6 -> x0, other arithmetic: 47 us -> none  [the longest x2 29.8 us: aperture_slowness(): jnp.sum(jnp.where(window[None] == levels[:, None, None], slowness_table[:...]
    while x55 -> x0, local copies, waits for them, and re-layouts: 45 us -> none
    another operation x21 -> x2, other arithmetic: 45.5 us -> 3.33 us  [shards(): jnp.stack([lax.dynamic_slice(slowness_codes[0], (anchors[s, 0], anchors[s...]
    add x2 -> x0, other arithmetic: 31.9 us -> none  [record_shot(): return record + correlate(padded[:, :, 0], padded[:, :, 1], rows_x)]
  transfers between devices with their start and end apart: 4 -> 1, of which waited for: 4 -> 1; matrix products, arithmetic and copies ran while one was open for 0% -> 0% of each run, Pallas kernels for 0% -> 0%
where the time goes in v1:
time: 239 us; the launch traced here: 238 us
  Pallas kernels  164 us (69%)
  waiting for transfers between devices  47.3 us (20%)
  between operations  21 us (9%)
  other arithmetic  3.33 us (1%)
  local copies, waits for them, and re-layouts  3.28 us (1%)
    pallas_call x1, Pallas kernels, make_image(): pl.pallas_call(functools.partial(image_kernel, factor), out_shape=jax.Sha...  110 us
    pallas_call x1, Pallas kernels, make_fields(): pl.pallas_call(fields_kernel, out_shape=jax.ShapeDtypeStruct((2, 2, 2, 4,...  53.8 us
    all_gather x1, waiting for transfers between devices, shards(): windows = lax.all_gather(windows, 'depth')  47.2 us
  transfers between devices with their start and end apart: 1, of which 1 were waited for; matrix products, arithmetic and copies ran while one was open for 0% of the time, Pallas kernels for 0%

profile of v1, /device:TPU:8, one launch (start us, length us, event | category | flops | bytes accessed | tf_op | source)
XLA Modules:
  0.0 238.4 jit_solution(2059560729543298316)
XLA Ops:
  6.5 0.0 all-gather.2.cloned.1.call-start
  6.5 1.4 fusion.2
  15.5 2.3 fusion
  17.8 1.1 pad_maximum_fusion
  18.8 0.0 all-gather.2.cloned.1.call-update
  18.9 47.2 %all-gather.2.cloned.1.call-done.codes = bf16[4,2,512,512]{3,2,1,0:T(8,128)(2,1)} async-done(((bf16[1,2,512,512]{3,2,1,0:T(8,128)(2,1)}), bf16[4,2,512,512]{3,2,1,0:T(8,128)(2,1)}) %all-gather.2.cloned.1.call-update) | async-done | bytes 4194320 | tf_op jit(solution)/shard_map/all_gather | solution.py:419
  66.1 53.8 %fields.1 = bf16[2,2,2,4,512,128]{5,4,3,2,1,0:T(8,128)(2,1)} custom-call(bf16[2,1,2,512,512]{4,3,2,1,0:T(8,128)(2,1)} %src.1, bf16[2,1,2,512,512]{4,3,2,1,0:T(8,128)(2,1)} %rec.1, bf16[4,2,512,512]{3,2,1,0:T(8,128)(2,1)} %all-gather.2.cloned.1.call-done.codes, f32[32]{0:T(128)} %table.1, bf16[4,256,256]{2,1,0:T(8,128)(2,1)} %constant.10.clone.right_ref, ...), custom_call_target="tpu_custom_call" | custom-call | tf_op jit(solution)/shard_map/fields/pallas_call | solution.py:244
  119.9 109.7 %image.1 = f32[15,16,512]{2,1,0:T(8,128)} custom-call(bf16[2,2,2,4,512,128]{5,4,3,2,1,0:T(8,128)(2,1)} %fields.1), custom_call_target="tpu_custom_call" | custom-call | tf_op jit(solution)/shard_map/image/pallas_call | solution.py:385
  229.7 1.9 copy.9
Async XLA Ops:
  6.5 59.6 %all-gather.2.cloned.1.call-start = ((), (), s32[]{:S(2)}) async-start(), calls=%async_computation | async-start | bytes 5242880 | tf_op jit(solution)/shard_map/all_gather | solution.py:419
Sparse Core Ops, SparseCore 0:
  19.0 47.0 all-gather.1

commit v2 on v1

--- a/solution.py
+++ b/solution.py
@@ -64,8 +64,170 @@
     return (er + fr, dr - gi, er - fr, dr + gi), (ei + fi, di + gr, ei - fi, di - gr)
 
 
+def level_row(table):
+    lane = lax.broadcasted_iota(jnp.int32, (8, B), 1)
+    levels = jnp.zeros((8, B), F32)
+    for k in range(32):
+        levels = jnp.where(lane == k, table[k], levels)
+    return levels
+
+
+TAKE = lax.GatherDimensionNumbers(
+    offset_dims=(), collapsed_slice_dims=(1,), start_index_map=(1,),
+    operand_batching_dims=(0,), start_indices_batching_dims=(0,))
+
+
+def lookup(values, index):
+    return lax.gather(
+        jnp.tile(values, (index.shape[0] // 8, 1)), index[..., None], TAKE, (1, 1),
+        mode=lax.GatherScatterMode.PROMISE_IN_BOUNDS)
+
+
+def windows_kernel(codes, table, anchors, out, means, raw, sem):
+    def fetch(s, h):
+        ox = pl.multiple_of(anchors[s, 0], N)
+        oy = pl.multiple_of(anchors[s, 1], N)
+        return pltpu.make_async_copy(
+            codes.at[0, pl.ds(ox + h * 256, 256), pl.ds(oy, N)], raw.at[s, h], sem.at[s, h])
+
+    for s in range(2):
+        for h in range(2):
+            fetch(s, h).start()
+    levels = level_row(table)
+    for s in range(2):
+        total = jnp.zeros((8, B), F32)
+        for h in range(2):
+            fetch(s, h).wait()
+
+            def rows_of(n, total):
+                take = pl.ds(pl.multiple_of(n * 32, 32), 32)
+                for q in range(4):
+                    index = raw[s, h, take, q * B:(q + 1) * B]
+                    out[s, pl.ds(pl.multiple_of(h * 256 + n * 32, 32), 32), q * B:(q + 1) * B] = (
+                        index.astype(F32).astype(BF16))
+                    got = lookup(levels, index)
+                    total = total + (got[0:8] + got[8:16]) + (got[16:24] + got[24:32])
+                return total
+
+            total = lax.fori_loop(0, 8, rows_of, total)
+        means[s] = jnp.full((8, B), jnp.sum(total) * (1.0 / (N * N)), F32)
+
+
+def make_windows(codes, table, anchors):
+    vmem = pl.BlockSpec(memory_space=pltpu.VMEM)
+    smem = pl.BlockSpec(memory_space=pltpu.SMEM)
+    return pl.pallas_call(
+        windows_kernel,
+        out_shape=(
+            jax.ShapeDtypeStruct((2, N, N), BF16),
+            jax.ShapeDtypeStruct((2, 8, B), F32),
+        ),
+        in_specs=[pl.BlockSpec(memory_space=pl.ANY), smem, smem],
+        out_specs=(vmem, vmem),
+        scratch_shapes=[pltpu.VMEM((2, 2, 256, N), jnp.int32), pltpu.SemaphoreType.DMA((2, 2))],
+        compiler_params=pltpu.CompilerParams(vmem_limit_bytes=32 * 1024 * 1024),
+        name="windows",
+    )(codes, table, anchors)
+
+
+def exchange_kernel(win, means, out, outm, lsem, ssem, rsem, msend, mrecv):
+    depth = lax.axis_index("depth")
+    freq = lax.axis_index("freq")
+    core = depth % 2
+    section = depth // 2
+    flipped = (freq + 16) % 32
+    sibling = (depth + 1 - 2 * core, freq)
+    half = N // 2
+    up = lambda s: (2 * (1 - section) + s, freq)
+    down = lambda s: (2 * (1 - section) + s, flipped)
+
+    barrier = pltpu.get_barrier_semaphore()
+    for who in (sibling, up(0), up(1), down(0), down(1)):
+        pl.semaphore_signal(barrier, inc=1, device_id=who, device_id_type=MESH)
+    pl.semaphore_wait(barrier, 5)
+
+    def to_section(s, way):
+        rows = pl.ds(way * half, half)
+        who = (up(s), down(s))[way]
+        return (
+            pltpu.make_async_remote_copy(
+                src_ref=win.at[s, rows], dst_ref=out.at[core, rows],
+                send_sem=ssem.at[s, way], recv_sem=rsem.at[core, way],
+                device_id=who, device_id_type=MESH),
+        )
+
+    def means_to_section(s):
+        return pltpu.make_async_remote_copy(
+            src_ref=means.at[s], dst_ref=outm.at[core],
+            send_sem=msend.at[s], recv_sem=mrecv.at[core],
+            device_id=up(s), device_id_type=MESH)
+
+    @pl.when(section == 0)
+    def _():
+        for s in range(2):
+            means_to_section(s).start()
+            for way in range(2):
+                for copy in to_section(s, way):
+                    copy.start()
+
+    swap = pltpu.make_async_remote_copy(
+        src_ref=win.at[1 - core], dst_ref=out.at[depth],
+        send_sem=ssem.at[2, 0], recv_sem=rsem.at[2, 0], device_id=sibling, device_id_type=MESH)
+    swap.start()
+    swap_means = pltpu.make_async_remote_copy(
+        src_ref=means.at[1 - core], dst_ref=outm.at[depth],
+        send_sem=msend.at[2], recv_sem=mrecv.at[2], device_id=sibling, device_id_type=MESH)
+    swap_means.start()
+    keep = pltpu.make_async_copy(win.at[core], out.at[depth], lsem)
+    keep.start()
+    outm[depth] = means[core]
+    keep.wait()
+
+    swap.wait()
+    swap_means.wait()
+
+    @pl.when(section == 0)
+    def _():
+        for s in range(2):
+            means_to_section(s).wait_send()
+            for way in range(2):
+                for copy in to_section(s, way):
+                    copy.wait_send()
+
+    @pl.when(section == 1)
+    def _():
+        for plane in range(2):
+            pltpu.make_async_copy(outm.at[plane], outm.at[plane], mrecv.at[plane]).wait()
+            for way in range(2):
+                rows = pl.ds(way * half, half)
+                pltpu.make_async_copy(out.at[plane, rows], out.at[plane, rows], rsem.at[plane, way]).wait()
+
+
+def exchange(win, means):
+    vmem = pl.BlockSpec(memory_space=pltpu.VMEM)
+    return pl.pallas_call(
+        exchange_kernel,
+        out_shape=(
+            jax.ShapeDtypeStruct((4, N, N), BF16),
+            jax.ShapeDtypeStruct((4, 8, B), F32),
+        ),
+        in_specs=[vmem, vmem],
+        out_specs=(vmem, vmem),
+        scratch_shapes=[
+            pltpu.SemaphoreType.DMA,
+            pltpu.SemaphoreType.DMA((3, 2)),
+            pltpu.SemaphoreType.DMA((3, 2)),
+            pltpu.SemaphoreType.DMA((3,)),
+            pltpu.SemaphoreType.DMA((3,)),
+        ],
+        compiler_params=pltpu.CompilerParams(
+            collective_id=2, has_side_effects=True, vmem_limit_bytes=16 * 1024 * 1024),
+        name="exchange",
+    )(win, means)
+
+
 def fields_kernel(
-    src, rec, codes, table, right_ref, left_ref, out,
+    src, rec, codes, sums, table, right_ref, left_ref, out,
     u, a, cbuf, ph, sc, tsem, csem, osem,
 ):
     depth = lax.axis_index("depth")
@@ -83,62 +245,51 @@
     for copy in tops:
         copy.start()
     for z in range(4):
-        pltpu.make_async_copy(codes.at[z, core], cbuf.at[z], csem.at[z]).start()
-
-    lane = lax.broadcasted_iota(jnp.int32, (8, B), 1)
-    levels = jnp.zeros((8, B), F32)
-    for k in range(32):
-        levels = jnp.where(lane == k, table[k], levels)
-
-    def lookup(values, index):
-        return jnp.take_along_axis(jnp.tile(values, (index.shape[0] // 8, 1)), index, axis=1)
+        pltpu.make_async_copy(codes.at[z], cbuf.at[z], csem.at[z]).start()
+
+    levels = level_row(table)
+    angle = angular * levels
+    squared = angle * angle
+    cos_levels = horner(COS_Q, squared)
+    sin_levels = angle * horner(SIN_Q, squared)
 
     for copy in tops:
         copy.wait()
 
     def step(z, carry):
-        pltpu.make_async_copy(codes.at[z, core], cbuf.at[z], csem.at[z]).wait()
-
-        def add_rows(i, total):
+        pltpu.make_async_copy(codes.at[z], cbuf.at[z], csem.at[z]).wait()
+        base = sums[z, 0:1, :]
+        turn = angular * base
+        turn_sq = turn * turn
+        turn_re = horner(COS_Q, turn_sq)
+        turn_im = turn * horner(SIN_Q, turn_sq)
+
+        def operators(n, carry):
+            rows = n * 24
+            k = rows + lax.broadcasted_iota(jnp.int32, (24, B), 0)
+            kx = (k % B) * 4 + k // B
+            kx = jnp.where(kx < N // 2, kx, kx - N).astype(F32) * (2.0 * math.pi / N)
+            left_q = turn_sq - kx * kx
+            for ry in range(3):
+                ky = lax.broadcasted_iota(jnp.int32, (1, B), 1) * 4 + ry
+                ky = jnp.where(ky < N // 2, ky, ky - N).astype(F32) * (2.0 * math.pi / N)
+                q = left_q - ky * ky
+                root = jnp.sqrt(jnp.abs(q))
+                wave = jnp.maximum(q, 0.0)
+                travels = q >= 0.0
+                pre = jnp.where(travels, horner(COS_Q, wave), jnp.exp(-root))
+                pim = jnp.where(travels, root * horner(SIN_Q, wave), 0.0)
+                put = pl.ds(pl.multiple_of(rows, 8), 24)
+                ph[0, ry, put, :] = pre * turn_re + pim * turn_im
+                ph[1, ry, put, :] = pim * turn_re - pre * turn_im
+            take = pl.ds(pl.multiple_of(n * 32, 32), 32)
             for q in range(4):
-                index = cbuf[z, pl.ds(i * 32, 32), q * B:(q + 1) * B].astype(jnp.int32)
-                got = lookup(levels, index)
-                total = total + (got[0:8] + got[8:16]) + (got[16:24] + got[24:32])
-            return total
-
-        total = lax.fori_loop(0, N // 32, add_rows, jnp.zeros((8, B), F32))
-        base = jnp.sum(total) * (1.0 / (N * N))
-
-        def phase_block(n, carry):
-            rx, ry = n // 3, n % 3
-            kx = lax.broadcasted_iota(jnp.int32, (B, B), 0) * 4 + rx
-            ky = lax.broadcasted_iota(jnp.int32, (B, B), 1) * 4 + ry
-            kx = jnp.where(kx < N // 2, kx, kx - N).astype(F32) * (2.0 * math.pi / N)
-            ky = jnp.where(ky < N // 2, ky, ky - N).astype(F32) * (2.0 * math.pi / N)
-            q = (angular * base) ** 2 - kx * kx - ky * ky
-            root = jnp.sqrt(jnp.abs(q))
-            decay = jnp.exp(-root)
-            wave = jnp.maximum(q, 0.0)
-            ph[0, rx, ry] = jnp.where(q >= 0.0, horner(COS_Q, wave), decay)
-            ph[1, rx, ry] = jnp.where(q >= 0.0, root * horner(SIN_Q, wave), 0.0)
+                index = cbuf[z, take, q * B:(q + 1) * B].astype(jnp.int32)
+                sc[0, q, take, :] = lookup(cos_levels, index)
+                sc[1, q, take, :] = lookup(sin_levels, index)
             return carry
 
-        lax.fori_loop(0, 9, phase_block, 0)
-
-        angle = angular * (levels - base)
-        squared = angle * angle
-        cos_levels = horner(COS_Q, squared)
-        sin_levels = angle * horner(SIN_Q, squared)
-
-        def screen_rows(i, carry):
-            rows = pl.ds(i * 32, 32)
-            for q in range(4):
-                index = cbuf[z, rows, q * B:(q + 1) * B].astype(jnp.int32)
-                sc[0, q, rows, :] = lookup(cos_levels, index)
-                sc[1, q, rows, :] = lookup(sin_levels, index)
-            return carry
-
-        lax.fori_loop(0, N // 32, screen_rows, 0)
+        lax.fori_loop(0, 16, operators, 0)
 
         def wide(ref, kind, p, half, block):
             rows = slice(block * B, (block + 1) * B)
@@ -166,7 +317,7 @@
         def along_y(n, carry):
             kind, rx = n // 4, n % 4
             sign = (1 - 2 * kind).astype(F32)
-            px = jnp.where(rx == 3, 1, rx)
+            prow = pl.ds(pl.multiple_of(jnp.where(rx == 3, 1, rx) * B, B), B)
             rows = pl.ds(pl.multiple_of(rx * B, B), B)
             re = [a[kind, 0, q, rows, :] for q in range(4)]
             im = [a[kind, 1, q, rows, :] for q in range(4)]
@@ -177,7 +328,7 @@
                               preferred_element_type=F32)
                 gre, gim = got[:, :B], got[:, B:]
                 py = 1 if r == 3 else r
-                pre, pim = ph[0, px, py], ph[1, px, py] * sign
+                pre, pim = ph[0, py, prow, :], ph[1, py, prow, :] * sign
                 turned = jnp.concatenate(
                     [(gre * pre - gim * pim).astype(BF16), (gre * pim + gim * pre).astype(BF16)], axis=1)
                 back = jnp.dot(turned, left_ref[r], preferred_element_type=F32)
@@ -231,26 +382,26 @@
     lax.fori_loop(0, steps, step, 0)
 
     def drain(z, carry):
-        pltpu.make_async_copy(codes.at[z, core], cbuf.at[z], csem.at[z]).wait()
+        pltpu.make_async_copy(codes.at[z], cbuf.at[z], csem.at[z]).wait()
         return carry
 
     lax.fori_loop(steps, 4, drain, 0)
     pltpu.make_async_copy(u, out.at[1], osem.at[1]).wait()
 
 
-def make_fields(src, rec, codes, table, right, left):
+def make_fields(src, rec, codes, sums, table, right, left):
     vmem = pl.BlockSpec(memory_space=pltpu.VMEM)
     hbm = pl.BlockSpec(memory_space=pl.ANY)
     return pl.pallas_call(
         fields_kernel,
         out_shape=jax.ShapeDtypeStruct((2, 2, 2, 4, N, B), BF16),
-        in_specs=[hbm, hbm, hbm, pl.BlockSpec(memory_space=pltpu.SMEM), vmem, vmem],
+        in_specs=[hbm, hbm, hbm, vmem, pl.BlockSpec(memory_space=pltpu.SMEM), vmem, vmem],
         out_specs=hbm,
         scratch_shapes=[
             pltpu.VMEM((2, 2, 4, N, B), BF16),
             pltpu.VMEM((2, 2, 4, N, B), BF16),
             pltpu.VMEM((4, N, N), BF16),
-            pltpu.VMEM((2, 3, 3, B, B), F32),
+            pltpu.VMEM((2, 3, 3 * B, B), F32),
             pltpu.VMEM((2, 4, N, B), F32),
             pltpu.SemaphoreType.DMA((2, 4)),
             pltpu.SemaphoreType.DMA((4,)),
@@ -258,7 +409,7 @@
         ],
         compiler_params=pltpu.CompilerParams(vmem_limit_bytes=60 * 1024 * 1024),
         name="fields",
-    )(src, rec, codes, table, right, left)
+    )(src, rec, codes, sums, table, right, left)
 
 
 def image_kernel(factor, fields, out, own, other, pad, buf, r0, r1, r2, r3, r4,
@@ -313,30 +464,31 @@
 
     mine = bits(x, z)
 
+    flip_x = [[(mine[d] + bits(v, 0)[d]) % 2 for d in range(2)] for v in range(4)]
+    slot_x = [[sum(flip_x[v][d] * (16 >> ((d - i) % 4)) for d in range(2)) for i in range(4)] for v in range(4)]
+
     def produce(g):
         def body(n, carry):
-            i, f = n // 32, n % 32
-            theirs = bits(f % 4, (f // 4) % 4)
-            rel = [(m + t) % 2 for m, t in zip(mine, theirs)]
-            ybit = (yh + f // 16) % 2
-            slot = ybit
-            for t in range(4):
-                d = (i + t) % 4
-                pick = jnp.where(d == 0, rel[0], jnp.where(d == 1, rel[1], jnp.where(d == 2, rel[2], rel[3])))
-                slot = slot + pick * (16 >> t)
-            row = f * 16
-            for l in range(PER):
-                h = g * PER + l - LAG
-                total = None
-                for s in range(2):
-                    for p in range(2):
-                        left = pad[s, 0, p, i, pl.ds(row + (8 - h), 16), :]
-                        right = pad[s, 1, p, i, pl.ds(row + (8 + h), 16), :]
-                        term = left * right
-                        total = term if total is None else total + term
-                buf[g, i, slot, l] = total.astype(BF16)
+            theirs = bits(0, n % 4)
+            flip_z = [(mine[d] + theirs[d]) % 2 for d in (2, 3)]
+            last = (yh + n // 4) % 2
+            slot_z = [last + sum(flip_z[d - 2] * (16 >> ((d - i) % 4)) for d in (2, 3)) for i in range(4)]
+            for v in range(4):
+                row = pl.multiple_of(n * 64 + v * 16, 16)
+                for i in range(4):
+                    slot = slot_z[i] + slot_x[v][i]
+                    for l in range(PER):
+                        h = g * PER + l - LAG
+                        total = None
+                        for s in range(2):
+                            for p in range(2):
+                                left = pad[s, 0, p, i, pl.ds(row + (8 - h), 16), :]
+                                right = pad[s, 1, p, i, pl.ds(row + (8 + h), 16), :]
+                                term = left * right
+                                total = term if total is None else total + term
+                        buf[g, i, slot, l] = total.astype(BF16)
             return carry
-        lax.fori_loop(0, 128, body, 0)
+        lax.fori_loop(0, 8, body, 0)
 
     recv = (r0, r1, r2, r3, r4)
 
@@ -413,11 +565,9 @@
     right, left = butterfly_matrices()
     right = jnp.asarray(right, BF16)
     left = jnp.asarray(left, BF16)
-    windows = jnp.stack([
-        lax.dynamic_slice(slowness_codes[0], (anchors[s, 0], anchors[s, 1]), (N, N)) for s in range(2)
-    ]).astype(BF16)
-    windows = lax.all_gather(windows, "depth")
-    fields = make_fields(source_top, receiver_top, windows, slowness_table, right, left)
+    windows, means = make_windows(slowness_codes, slowness_table, anchors)
+    codes, sums = exchange(windows, means)
+    fields = make_fields(source_top, receiver_top, codes, sums, slowness_table, right, left)
     image = make_image(fields, 1.0 / math.sqrt(128.0))
     return image[None]
 

time: 239 us -> 142 us (0.59)
  waiting for transfers between devices: 47.3 us -> 0 us
  Pallas kernels: 164 us -> 134 us
  between operations: 21 us -> 0.05 us
  local copies, waits for them, and re-layouts: 3.28 us -> 7.28 us
  other arithmetic: 3.33 us -> 0 us
    all_gather x1 -> x0, waiting for transfers between devices: 47.2 us -> none  [shards(): windows = lax.all_gather(windows, 'depth')]
    pallas_call x1, Pallas kernels: 110 us -> 77.5 us  [make_image(): pl.pallas_call(functools.partial(image_kernel, factor), out_shape=jax.Sha...]
    pallas_call x0 -> x2, Pallas kernels: none -> 15.6 us  [the longest x1 11 us: exchange(): pl.pallas_call(exchange_kernel, out_shape=(jax.ShapeDtypeStruct((4, N, N)...]
    pallas_call x1, Pallas kernels: 53.8 us -> 41.2 us  [make_fields(): pl.pallas_call(fields_kernel, out_shape=jax.ShapeDtypeStruct((2, 2, 2, 4,...]
    unnamed x1 -> x11, local copies, waits for them, and re-layouts: 1.85 us -> 7.28 us
    another operation x2 -> x0, other arithmetic: 3.33 us -> none  [shards(): jnp.stack([lax.dynamic_slice(slowness_codes[0], (anchors[s, 0], anchors[s...]
  transfers between devices with their start and end apart: 1 -> 0, of which waited for: 1 -> 0; matrix products, arithmetic and copies ran while one was open for 0% -> 0% of each run, Pallas kernels for 0% -> 0%
where the time goes in v2:
time: 142 us
  Pallas kernels  134 us (94%)
  local copies, waits for them, and re-layouts  7.28 us (5%)
    pallas_call x1, Pallas kernels, make_image(): pl.pallas_call(functools.partial(image_kernel, factor), out_shape=jax.Sha...  77.5 us
    pallas_call x1, Pallas kernels, make_fields(): pl.pallas_call(fields_kernel, out_shape=jax.ShapeDtypeStruct((2, 2, 2, 4,...  41.2 us
    pallas_call x1, Pallas kernels, exchange(): pl.pallas_call(exchange_kernel, out_shape=(jax.ShapeDtypeStruct((4, N, N)...  11 us
    unnamed x11, local copies, waits for them, and re-layouts  7.28 us
    pallas_call x1, Pallas kernels, make_windows(): pl.pallas_call(windows_kernel, out_shape=(jax.ShapeDtypeStruct((2, N, N),...  4.57 us

profile of v2, /device:TPU:8, one launch (start us, length us, event | category | flops | bytes accessed | tf_op | source)
XLA Modules:
  0.0 141.5 jit_solution(8176268171140987317)
XLA Ops:
  0.0 0.0 copy-start
  0.0 2.2 %copy-done = s32[1,1024,1024]{2,1,0:T(8,128)S(1)} copy-done((s32[1,1024,1024]{2,1,0:T(8,128)S(1)}, s32[1,1024,1024]{2,1,0:T(8,128)}, u32[]{:S(2)}) %copy-start) | copy-done | bytes 4194328
  2.2 0.0 copy-start.3
  2.2 0.7 copy-done.3
  2.8 0.0 copy-start.4
  2.8 0.7 copy-done.4
  3.5 4.6 %windows.1 = (bf16[2,512,512]{2,1,0:T(8,128)(2,1)S(1)}, f32[2,8,128]{2,1,0:T(8,128)S(1)}) custom-call(s32[1,1024,1024]{2,1,0:T(8,128)S(1)} %copy-done, f32[32]{0:T(128)S(1)} %copy-done.3, s32[2,2]{1,0:T(2,128)S(1)} %copy-done.4), custom_call_target="tpu_custom_call" | custom-call | tf_op jit(solution)/shard_map/windows/pallas_call | solution.py:119
  8.1 11.0 %exchange.1 = (bf16[4,512,512]{2,1,0:T(8,128)(2,1)S(1)}, f32[4,8,128]{2,1,0:T(8,128)S(1)}) custom-call(bf16[2,512,512]{2,1,0:T(8,128)(2,1)S(1)} %get-tuple-element.9.win, f32[2,8,128]{2,1,0:T(8,128)S(1)} %get-tuple-element.10.means), custom_call_target="tpu_custom_call" | custom-call | tf_op jit(solution)/shard_map/exchange/pallas_call | solution.py:208
  19.1 0.0 copy-start.1
  19.1 1.3 copy-done.1
  20.4 0.0 copy-start.2
  20.4 0.6 copy-done.2
  21.0 41.2 %fields.1 = bf16[2,2,2,4,512,128]{5,4,3,2,1,0:T(8,128)(2,1)} custom-call(bf16[2,1,2,512,512]{4,3,2,1,0:T(8,128)(2,1)} %src.1, bf16[2,1,2,512,512]{4,3,2,1,0:T(8,128)(2,1)} %rec.1, bf16[4,512,512]{2,1,0:T(8,128)(2,1)} %copy-done.1, f32[4,8,128]{2,1,0:T(8,128)} %copy-done.2, f32[32]{0:T(128)} %table.3, bf16[4,256,256]{2,1,0:T(8,128)(2,1)} %constant.4.clone.right_ref, ...), custom_call_target="tpu_custom_call" | custom-call | tf_op jit(solution)/shard_map/fields/pallas_call | solution.py:395
  62.2 77.5 %image.1 = f32[15,16,512]{2,1,0:T(8,128)} custom-call(bf16[2,2,2,4,512,128]{5,4,3,2,1,0:T(8,128)(2,1)} %fields.1), custom_call_target="tpu_custom_call" | custom-call | tf_op jit(solution)/shard_map/image/pallas_call | solution.py:537
  139.7 1.9 %copy.9 = f32[1,15,16,512]{3,2,1,0:T(8,128)} copy(f32[1,15,16,512]{3,2,1,0:T(8,128)} %bitcast.1) | data formatting | bytes 983040
Async XLA Ops:
  0.0 2.2 %copy-start = (s32[1,1024,1024]{2,1,0:T(8,128)S(1)}, s32[1,1024,1024]{2,1,0:T(8,128)}, u32[]{:S(2)}) copy-start(s32[1,1024,1024]{2,1,0:T(8,128)} %codes.1) | copy-start | bytes 12582916
  2.2 0.7 copy-start.3
  2.8 0.7 copy-start.4
  19.1 1.3 copy-start.1
  20.4 0.6 copy-start.2

commit v3 on v2

--- a/solution.py
+++ b/solution.py
@@ -125,7 +125,7 @@
         in_specs=[pl.BlockSpec(memory_space=pl.ANY), smem, smem],
         out_specs=(vmem, vmem),
         scratch_shapes=[pltpu.VMEM((2, 2, 256, N), jnp.int32), pltpu.SemaphoreType.DMA((2, 2))],
-        compiler_params=pltpu.CompilerParams(vmem_limit_bytes=32 * 1024 * 1024),
+        compiler_params=pltpu.CompilerParams(vmem_limit_bytes=60 * 1024 * 1024),
         name="windows",
     )(codes, table, anchors)
 
@@ -221,7 +221,7 @@
             pltpu.SemaphoreType.DMA((3,)),
         ],
         compiler_params=pltpu.CompilerParams(
-            collective_id=2, has_side_effects=True, vmem_limit_bytes=16 * 1024 * 1024),
+            collective_id=2, has_side_effects=True, vmem_limit_bytes=60 * 1024 * 1024),
         name="exchange",
     )(win, means)
 
@@ -412,123 +412,181 @@
     )(src, rec, codes, sums, table, right, left)
 
 
-def image_kernel(factor, fields, out, own, other, pad, buf, r0, r1, r2, r3, r4,
-                 lsem, ssem, rsem, xs, xr):
+def image_kernel(factor, fields, out, raw, pad, buf, r1, r2, r3, fa, fb,
+                 lsem, esend, erecv, ssem, rsem, fsend, frecv):
     depth = lax.axis_index("depth")
     freq = lax.axis_index("freq")
     core = depth % 2
+    other = depth + 1 - 2 * core
     x, z, yh = freq % 4, (freq // 4) % 4, freq // 16
-    base = yh * 16 + z * 4 + x
-    sibling = (depth + 1 - 2 * core, freq)
-    dims = (
-        (depth, base - x + (x + 1 - 2 * (x % 2))),
-        (depth, base - x + (3 - x)),
-        (depth, base - 4 * z + 4 * (z + 1 - 2 * (z % 2))),
-        (depth, base - 4 * z + 4 * (3 - z)),
+    ring = (
+        freq - x + (x + 1 - 2 * (x % 2)),
+        freq - x + (3 - x),
+        freq - 4 * z + 4 * (z + 1 - 2 * (z % 2)),
+        freq - 4 * z + 4 * (3 - z),
     )
-    across = (depth, base - 16 * yh + 16 * (1 - yh))
+    far = freq - 16 * yh + 16 * (1 - yh)
+    far_ring = [r - 16 * yh + 16 * (1 - yh) for r in ring]
+
+    def bits(ix, iz):
+        return [((ix + 1) // 2) % 2, ix // 2, ((iz + 1) // 2) % 2, iz // 2]
+
+    mine = bits(x, z)
 
     barrier = pltpu.get_barrier_semaphore()
-    for who in (sibling, across) + dims:
+    peers = [(other, freq), (depth, far)]
+    for i in range(4):
+        peers += [(depth, ring[i]), (other, ring[i]), (depth, far_ring[i])]
+    for who in peers:
         pl.semaphore_signal(barrier, inc=1, device_id=who, device_id_type=MESH)
-    local = pltpu.make_async_copy(fields.at[core], own, lsem)
-    local.start()
-    pl.semaphore_wait(barrier, 6)
-    swap = pltpu.make_async_remote_copy(
-        src_ref=fields.at[1 - core], dst_ref=other, send_sem=xs, recv_sem=xr,
-        device_id=sibling, device_id_type=MESH)
-    swap.start()
-
-    for s in range(2):
+
+    def window(i, side):
+        return pl.ds(pl.multiple_of(side * 240, 16), 272)
+
+    def keep(i):
+        return pltpu.make_async_copy(
+            fields.at[core, :, :, i, window(i, mine[i])], raw.at[i, 0], lsem.at[i])
+
+    def hand(i, n):
+        plane = (1 - core, core, 1 - core)[n]
+        side = (mine[i], 1 - mine[i], 1 - mine[i])[n]
+        who = ((other, freq), (depth, ring[i]), (other, ring[i]))[n]
+        return pltpu.make_async_remote_copy(
+            src_ref=fields.at[plane, :, :, i, window(i, side)], dst_ref=raw.at[i, n + 1],
+            send_sem=esend.at[i, n], recv_sem=erecv.at[i, n],
+            device_id=who, device_id_type=MESH)
+
+    for i in range(4):
+        keep(i).start()
+    pl.semaphore_wait(barrier, len(peers))
+    for n in (1, 2, 0):
+        for i in range(4):
+            hand(i, n).start()
+
+    for i in range(4):
+        for s in range(4):
+            for k in range(2):
+                for p in range(2):
+                    pad[i, s, k, p, 0:8, :] = jnp.zeros((8, B), F32)
+                    pad[i, s, k, p, 280:288, :] = jnp.zeros((8, B), F32)
+
+    def widen(i, s):
         for k in range(2):
             for p in range(2):
-                for i in range(4):
-                    pad[s, k, p, i, 0:8, :] = jnp.zeros((8, B), F32)
-                    pad[s, k, p, i, N + 8:N + 16, :] = jnp.zeros((8, B), F32)
-
-    def widen(s, ref):
-        def body(n, carry):
-            k, p, i = n // 8, (n // 4) % 2, n % 4
-            for h in range(2):
-                pad[s, k, p, i, 8 + h * 256:8 + (h + 1) * 256, :] = ref[k, p, i, h * 256:(h + 1) * 256, :].astype(F32)
-            return carry
-        lax.fori_loop(0, 16, body, 0)
-
-    local.wait()
-    widen(0, own)
-    swap.wait()
-    widen(1, other)
-
-    def bits(ix, iz):
-        return [((ix + 1) // 2) % 2, ix // 2, ((iz + 1) // 2) % 2, iz // 2]
-
-    mine = bits(x, z)
+                pad[i, s, k, p, 8:280, :] = raw[i, s, k, p].astype(F32)
+
+    for i in range(4):
+        keep(i).wait()
+        widen(i, 0)
+    for n in range(3):
+        for i in range(4):
+            hand(i, n).wait_recv()
+            widen(i, n + 1)
+
+    def weight(d, i):
+        return (1, 8, 4, 2)[(d - i) % 4]
 
     flip_x = [[(mine[d] + bits(v, 0)[d]) % 2 for d in range(2)] for v in range(4)]
-    slot_x = [[sum(flip_x[v][d] * (16 >> ((d - i) % 4)) for d in range(2)) for i in range(4)] for v in range(4)]
+    slot_x = [[sum(flip_x[v][d] * weight(d, i) for d in range(2)) for i in range(4)] for v in range(4)]
+    shift = [mine[i] * 16 for i in range(4)]
 
     def produce(g):
         def body(n, carry):
-            theirs = bits(0, n % 4)
+            theirs = bits(0, n)
             flip_z = [(mine[d] + theirs[d]) % 2 for d in (2, 3)]
-            last = (yh + n // 4) % 2
-            slot_z = [last + sum(flip_z[d - 2] * (16 >> ((d - i) % 4)) for d in (2, 3)) for i in range(4)]
+            slot_z = [sum(flip_z[d - 2] * weight(d, i) for d in (2, 3)) for i in range(4)]
             for v in range(4):
-                row = pl.multiple_of(n * 64 + v * 16, 16)
                 for i in range(4):
+                    row = pl.multiple_of(n * 64 + v * 16 + shift[i], 16)
                     slot = slot_z[i] + slot_x[v][i]
                     for l in range(PER):
                         h = g * PER + l - LAG
                         total = None
-                        for s in range(2):
+                        for s in range(4):
                             for p in range(2):
-                                left = pad[s, 0, p, i, pl.ds(row + (8 - h), 16), :]
-                                right = pad[s, 1, p, i, pl.ds(row + (8 + h), 16), :]
+                                left = pad[i, s, 0, p, pl.ds(row + (8 - h), 16), :]
+                                right = pad[i, s, 1, p, pl.ds(row + (8 + h), 16), :]
                                 term = left * right
                                 total = term if total is None else total + term
                         buf[g, i, slot, l] = total.astype(BF16)
             return carry
-        lax.fori_loop(0, 8, body, 0)
-
-    recv = (r0, r1, r2, r3, r4)
+        lax.fori_loop(0, 4, body, 0)
+
+    recv = (None, r1, r2, r3)
 
     def copy(g, i, t):
         half = 16 >> t
-        who = across if t == 4 else dims[(i + t) % 4]
         return pltpu.make_async_remote_copy(
             src_ref=buf.at[g, i, pl.ds(half, half)], dst_ref=recv[t].at[g, i],
-            send_sem=ssem.at[g, i, t], recv_sem=rsem.at[g, i, t],
+            send_sem=ssem.at[g, i, t - 1], recv_sem=rsem.at[g, i, t - 1],
+            device_id=(depth, ring[(i + t) % 4]), device_id_type=MESH)
+
+    def last(g, i, slot, who, place):
+        return pltpu.make_async_remote_copy(
+            src_ref=buf.at[g, i, slot], dst_ref=(fa, fb)[place].at[g, i],
+            send_sem=fsend.at[g, i, slot], recv_sem=frecv.at[g, i, place],
             device_id=who, device_id_type=MESH)
+
+    at_home = [mine[i] == yh for i in range(4)]
+
+    def sends_last(g, i, act):
+        @pl.when(at_home[i])
+        def _():
+            act(last(g, i, 1, (depth, ring[i]), 0))
+
+        @pl.when(jnp.logical_not(at_home[i]))
+        def _():
+            act(last(g, i, 0, (depth, far), 0))
+            act(last(g, i, 1, (depth, far_ring[i]), 1))
 
     def arrive(g, i, t):
         copy(g, i, t).wait_recv()
         half = 16 >> t
 
-        if t < 4:
-            def body(n, carry):
-                k = half - 1 - n
+        def body(n, carry):
+            for k in (half - 1 - 2 * n, half - 2 - 2 * n):
                 buf[g, i, k] = buf[g, i, k] + recv[t][g, i, k]
-                return carry
-            lax.fori_loop(0, half, body, 0)
+            return carry
+        lax.fori_loop(0, half // 2, body, 0)
+        if t < 3:
             copy(g, i, t + 1).start()
         else:
-            total = buf[g, i, 0].astype(F32) + recv[4][g, i, 0].astype(F32)
-            out[g * PER:(g + 1) * PER, :, i * B:(i + 1) * B] = total * factor
+            sends_last(g, i, lambda c: c.start())
+
+    def finish(g, i):
+        last(g, i, 0, (depth, far), 0).wait_recv()
+        put = (slice(g * PER, (g + 1) * PER), slice(None), slice(i * B, (i + 1) * B))
+
+        @pl.when(at_home[i])
+        def _():
+            out[put] = (buf[g, i, 0].astype(F32) + fa[g, i].astype(F32)) * factor
+
+        @pl.when(jnp.logical_not(at_home[i]))
+        def _():
+            last(g, i, 1, (depth, far_ring[i]), 1).wait_recv()
+            out[put] = (fa[g, i].astype(F32) + fb[g, i].astype(F32)) * factor
 
     for g in range(GROUPS):
         produce(g)
         for i in range(4):
-            copy(g, i, 0).start()
-    for w in range(GROUPS + 4):
-        for t in range(4, -1, -1):
+            copy(g, i, 1).start()
+    for w in range(1, GROUPS + 4):
+        for t in range(4, 0, -1):
             g = w - t
             if 0 <= g < GROUPS:
                 for i in range(4):
-                    arrive(g, i, t)
+                    if t == 4:
+                        finish(g, i)
+                    else:
+                        arrive(g, i, t)
+    for i in range(4):
+        for n in range(3):
+            hand(i, n).wait_send()
     for g in range(GROUPS):
         for i in range(4):
-            for t in range(5):
+            for t in (1, 2, 3):
                 copy(g, i, t).wait_send()
+            sends_last(g, i, lambda c: c.wait_send())
 
 
 def make_image(fields, factor):
@@ -540,20 +598,21 @@
         in_specs=[hbm],
         out_specs=pl.BlockSpec(memory_space=pltpu.VMEM),
         scratch_shapes=[
-            pltpu.VMEM((2, 2, 4, N, B), BF16),
-            pltpu.VMEM((2, 2, 4, N, B), BF16),
-            pltpu.VMEM((2, 2, 2, 4, N + 16, B), F32),
-            pltpu.VMEM((GROUPS, 4, 32) + strip, BF16),
+            pltpu.VMEM((4, 4, 2, 2, 272, B), BF16),
+            pltpu.VMEM((4, 4, 2, 2, 288, B), F32),
             pltpu.VMEM((GROUPS, 4, 16) + strip, BF16),
             pltpu.VMEM((GROUPS, 4, 8) + strip, BF16),
             pltpu.VMEM((GROUPS, 4, 4) + strip, BF16),
             pltpu.VMEM((GROUPS, 4, 2) + strip, BF16),
-            pltpu.VMEM((GROUPS, 4, 1) + strip, BF16),
-            pltpu.SemaphoreType.DMA,
-            pltpu.SemaphoreType.DMA((GROUPS, 4, 5)),
-            pltpu.SemaphoreType.DMA((GROUPS, 4, 5)),
-            pltpu.SemaphoreType.DMA,
-            pltpu.SemaphoreType.DMA,
+            pltpu.VMEM((GROUPS, 4) + strip, BF16),
+            pltpu.VMEM((GROUPS, 4) + strip, BF16),
+            pltpu.SemaphoreType.DMA((4,)),
+            pltpu.SemaphoreType.DMA((4, 3)),
+            pltpu.SemaphoreType.DMA((4, 3)),
+            pltpu.SemaphoreType.DMA((GROUPS, 4, 3)),
+            pltpu.SemaphoreType.DMA((GROUPS, 4, 3)),
+            pltpu.SemaphoreType.DMA((GROUPS, 4, 2)),
+            pltpu.SemaphoreType.DMA((GROUPS, 4, 2)),
         ],
         compiler_params=pltpu.CompilerParams(
             collective_id=1, has_side_effects=True, vmem_limit_bytes=60 * 1024 * 1024),

time: 142 us -> 135 us (0.951)
  local copies, waits for them, and re-layouts: 7.28 us -> 1.85 us
    pallas_call x1, Pallas kernels: 77.5 us -> 71.6 us  [make_image(): pl.pallas_call(functools.partial(image_kernel, factor), out_shape=jax.Sha...]
    unnamed x11 -> x1, local copies, waits for them, and re-layouts: 7.28 us -> 1.85 us
    pallas_call x1, Pallas kernels: 11 us -> 13.5 us  [exchange(): pl.pallas_call(exchange_kernel, out_shape=(jax.ShapeDtypeStruct((4, N, N)...]
    pallas_call x1, Pallas kernels: 4.57 us -> 6.31 us  [make_windows(): pl.pallas_call(windows_kernel, out_shape=(jax.ShapeDtypeStruct((2, N, N),...]
where the time goes in v3:
time: 135 us
  Pallas kernels  133 us (99%)
  local copies, waits for them, and re-layouts  1.85 us (1%)
    pallas_call x1, Pallas kernels, make_image(): pl.pallas_call(functools.partial(image_kernel, factor), out_shape=jax.Sha...  71.6 us
    pallas_call x1, Pallas kernels, make_fields(): pl.pallas_call(fields_kernel, out_shape=jax.ShapeDtypeStruct((2, 2, 2, 4,...  41.2 us
    pallas_call x1, Pallas kernels, exchange(): pl.pallas_call(exchange_kernel, out_shape=(jax.ShapeDtypeStruct((4, N, N)...  13.5 us
    pallas_call x1, Pallas kernels, make_windows(): pl.pallas_call(windows_kernel, out_shape=(jax.ShapeDtypeStruct((2, N, N),...  6.31 us

profile of v3, /device:TPU:8, one launch (start us, length us, event | category | flops | bytes accessed | tf_op | source)
XLA Modules:
  0.0 134.5 jit_solution(12956874495638716843)
XLA Ops:
  0.0 6.3 %windows.1 = (bf16[2,512,512]{2,1,0:T(8,128)(2,1)}, f32[2,8,128]{2,1,0:T(8,128)}) custom-call(s32[1,1024,1024]{2,1,0:T(8,128)} %codes.1, f32[32]{0:T(128)} %table.3, s32[2,2]{1,0:T(2,128)} %anchors.1), custom_call_target="tpu_custom_call" | custom-call | tf_op jit(solution)/shard_map/windows/pallas_call | solution.py:119
  6.3 13.5 %exchange.1 = (bf16[4,512,512]{2,1,0:T(8,128)(2,1)}, f32[4,8,128]{2,1,0:T(8,128)}) custom-call(bf16[2,512,512]{2,1,0:T(8,128)(2,1)} %get-tuple-element.9.win, f32[2,8,128]{2,1,0:T(8,128)} %get-tuple-element.10.means), custom_call_target="tpu_custom_call" | custom-call | tf_op jit(solution)/shard_map/exchange/pallas_call | solution.py:208
  19.8 41.2 %fields.1 = bf16[2,2,2,4,512,128]{5,4,3,2,1,0:T(8,128)(2,1)} custom-call(bf16[2,1,2,512,512]{4,3,2,1,0:T(8,128)(2,1)} %src.1, bf16[2,1,2,512,512]{4,3,2,1,0:T(8,128)(2,1)} %rec.1, bf16[4,512,512]{2,1,0:T(8,128)(2,1)} %get-tuple-element.11.codes, f32[4,8,128]{2,1,0:T(8,128)} %get-tuple-element.12.sums, f32[32]{0:T(128)} %table.3, ...), custom_call_target="tpu_custom_call" | custom-call | tf_op jit(solution)/shard_map/fields/pallas_call | solution.py:395
  61.0 71.6 %image.1 = f32[15,16,512]{2,1,0:T(8,128)} custom-call(bf16[2,2,2,4,512,128]{5,4,3,2,1,0:T(8,128)(2,1)} %fields.1), custom_call_target="tpu_custom_call" | custom-call | tf_op jit(solution)/shard_map/image/pallas_call | solution.py:595
  132.7 1.9 %copy.9 = f32[1,15,16,512]{3,2,1,0:T(8,128)} copy(f32[1,15,16,512]{3,2,1,0:T(8,128)} %bitcast.1) | data formatting | bytes 983040

commit v4 on v3

--- a/solution.py
+++ b/solution.py
@@ -432,6 +432,7 @@
         return [((ix + 1) // 2) % 2, ix // 2, ((iz + 1) // 2) % 2, iz // 2]
 
     mine = bits(x, z)
+    side = mine
 
     barrier = pltpu.get_barrier_semaphore()
     peers = [(other, freq), (depth, far)]
@@ -440,19 +441,19 @@
     for who in peers:
         pl.semaphore_signal(barrier, inc=1, device_id=who, device_id_type=MESH)
 
-    def window(i, side):
-        return pl.ds(pl.multiple_of(side * 240, 16), 272)
+    def window(i, half):
+        return pl.ds(pl.multiple_of(half * 240, 16), 272)
 
     def keep(i):
         return pltpu.make_async_copy(
-            fields.at[core, :, :, i, window(i, mine[i])], raw.at[i, 0], lsem.at[i])
+            fields.at[core, :, :, i, window(i, side[i])], raw.at[i, 0], lsem.at[i])
 
     def hand(i, n):
         plane = (1 - core, core, 1 - core)[n]
-        side = (mine[i], 1 - mine[i], 1 - mine[i])[n]
+        half = (side[i], 1 - side[i], 1 - side[i])[n]
         who = ((other, freq), (depth, ring[i]), (other, ring[i]))[n]
         return pltpu.make_async_remote_copy(
-            src_ref=fields.at[plane, :, :, i, window(i, side)], dst_ref=raw.at[i, n + 1],
+            src_ref=fields.at[plane, :, :, i, window(i, half)], dst_ref=raw.at[i, n + 1],
             send_sem=esend.at[i, n], recv_sem=erecv.at[i, n],
             device_id=who, device_id_type=MESH)
 
@@ -488,7 +489,7 @@
 
     flip_x = [[(mine[d] + bits(v, 0)[d]) % 2 for d in range(2)] for v in range(4)]
     slot_x = [[sum(flip_x[v][d] * weight(d, i) for d in range(2)) for i in range(4)] for v in range(4)]
-    shift = [mine[i] * 16 for i in range(4)]
+    shift = [side[i] * 16 for i in range(4)]
 
     def produce(g):
         def body(n, carry):
@@ -521,23 +522,23 @@
             send_sem=ssem.at[g, i, t - 1], recv_sem=rsem.at[g, i, t - 1],
             device_id=(depth, ring[(i + t) % 4]), device_id_type=MESH)
 
-    def last(g, i, slot, who, place):
+    def last(i, slot, who, place):
         return pltpu.make_async_remote_copy(
-            src_ref=buf.at[g, i, slot], dst_ref=(fa, fb)[place].at[g, i],
-            send_sem=fsend.at[g, i, slot], recv_sem=frecv.at[g, i, place],
+            src_ref=buf.at[:, i, slot], dst_ref=(fa, fb)[place].at[i],
+            send_sem=fsend.at[i, slot], recv_sem=frecv.at[i, place],
             device_id=who, device_id_type=MESH)
 
-    at_home = [mine[i] == yh for i in range(4)]
-
-    def sends_last(g, i, act):
+    at_home = [side[i] == yh for i in range(4)]
+
+    def sends_last(i, act):
         @pl.when(at_home[i])
         def _():
-            act(last(g, i, 1, (depth, ring[i]), 0))
+            act(last(i, 1, (depth, ring[i]), 0))
 
         @pl.when(jnp.logical_not(at_home[i]))
         def _():
-            act(last(g, i, 0, (depth, far), 0))
-            act(last(g, i, 1, (depth, far_ring[i]), 1))
+            act(last(i, 0, (depth, far), 0))
+            act(last(i, 1, (depth, far_ring[i]), 1))
 
     def arrive(g, i, t):
         copy(g, i, t).wait_recv()
@@ -550,35 +551,40 @@
         lax.fori_loop(0, half // 2, body, 0)
         if t < 3:
             copy(g, i, t + 1).start()
-        else:
-            sends_last(g, i, lambda c: c.start())
-
-    def finish(g, i):
-        last(g, i, 0, (depth, far), 0).wait_recv()
-        put = (slice(g * PER, (g + 1) * PER), slice(None), slice(i * B, (i + 1) * B))
+
+    def finish(i):
+        last(i, 0, (depth, far), 0).wait_recv()
+        cols = slice(i * B, (i + 1) * B)
 
         @pl.when(at_home[i])
         def _():
-            out[put] = (buf[g, i, 0].astype(F32) + fa[g, i].astype(F32)) * factor
+            for g in range(GROUPS):
+                out[g * PER:(g + 1) * PER, :, cols] = (buf[g, i, 0].astype(F32) + fa[i, g].astype(F32)) * factor
 
         @pl.when(jnp.logical_not(at_home[i]))
         def _():
-            last(g, i, 1, (depth, far_ring[i]), 1).wait_recv()
-            out[put] = (fa[g, i].astype(F32) + fb[g, i].astype(F32)) * factor
+            last(i, 1, (depth, far_ring[i]), 1).wait_recv()
+            for g in range(GROUPS):
+                out[g * PER:(g + 1) * PER, :, cols] = (fa[i, g].astype(F32) + fb[i, g].astype(F32)) * factor
 
     for g in range(GROUPS):
         produce(g)
         for i in range(4):
             copy(g, i, 1).start()
-    for w in range(1, GROUPS + 4):
-        for t in range(4, 0, -1):
-            g = w - t
-            if 0 <= g < GROUPS:
-                for i in range(4):
-                    if t == 4:
-                        finish(g, i)
-                    else:
-                        arrive(g, i, t)
+        if g >= 2:
+            for i in range(4):
+                arrive(g - 2, i, 1)
+    for g in range(GROUPS - 2, GROUPS):
+        for i in range(4):
+            arrive(g, i, 1)
+    for t in (2, 3):
+        for g in range(GROUPS):
+            for i in range(4):
+                arrive(g, i, t)
+                if t == 3 and g == GROUPS - 1:
+                    sends_last(i, lambda c: c.start())
+    for i in range(4):
+        finish(i)
     for i in range(4):
         for n in range(3):
             hand(i, n).wait_send()
@@ -586,7 +592,8 @@
         for i in range(4):
             for t in (1, 2, 3):
                 copy(g, i, t).wait_send()
-            sends_last(g, i, lambda c: c.wait_send())
+    for i in range(4):
+        sends_last(i, lambda c: c.wait_send())
 
 
 def make_image(fields, factor):
@@ -604,15 +611,15 @@
             pltpu.VMEM((GROUPS, 4, 8) + strip, BF16),
             pltpu.VMEM((GROUPS, 4, 4) + strip, BF16),
             pltpu.VMEM((GROUPS, 4, 2) + strip, BF16),
-            pltpu.VMEM((GROUPS, 4) + strip, BF16),
-            pltpu.VMEM((GROUPS, 4) + strip, BF16),
+            pltpu.VMEM((4, GROUPS) + strip, BF16),
+            pltpu.VMEM((4, GROUPS) + strip, BF16),
             pltpu.SemaphoreType.DMA((4,)),
             pltpu.SemaphoreType.DMA((4, 3)),
             pltpu.SemaphoreType.DMA((4, 3)),
             pltpu.SemaphoreType.DMA((GROUPS, 4, 3)),
             pltpu.SemaphoreType.DMA((GROUPS, 4, 3)),
-            pltpu.SemaphoreType.DMA((GROUPS, 4, 2)),
-            pltpu.SemaphoreType.DMA((GROUPS, 4, 2)),
+            pltpu.SemaphoreType.DMA((4, 2)),
+            pltpu.SemaphoreType.DMA((4, 2)),
         ],
         compiler_params=pltpu.CompilerParams(
             collective_id=1, has_side_effects=True, vmem_limit_bytes=60 * 1024 * 1024),

time: 135 us -> 122 us (0.904)
  Pallas kernels: 133 us -> 120 us
    pallas_call x1, Pallas kernels: 71.6 us -> 59.1 us  [make_image(): pl.pallas_call(functools.partial(image_kernel, factor), out_shape=jax.Sha...]
where the time goes in v4:
time: 122 us
  Pallas kernels  120 us (98%)
  local copies, waits for them, and re-layouts  1.85 us (2%)
    pallas_call x1, Pallas kernels, make_image(): pl.pallas_call(functools.partial(image_kernel, factor), out_shape=jax.Sha...  59.1 us
    pallas_call x1, Pallas kernels, make_fields(): pl.pallas_call(fields_kernel, out_shape=jax.ShapeDtypeStruct((2, 2, 2, 4,...  41.2 us
    pallas_call x1, Pallas kernels, exchange(): pl.pallas_call(exchange_kernel, out_shape=(jax.ShapeDtypeStruct((4, N, N)...  13.5 us
    pallas_call x1, Pallas kernels, make_windows(): pl.pallas_call(windows_kernel, out_shape=(jax.ShapeDtypeStruct((2, N, N),...  6.31 us

profile of v4, /device:TPU:8, one launch (start us, length us, event | category | flops | bytes accessed | tf_op | source)
XLA Modules:
  0.0 122.0 jit_solution(7265453410945034751)
XLA Ops:
  0.0 6.3 %windows.1 = (bf16[2,512,512]{2,1,0:T(8,128)(2,1)}, f32[2,8,128]{2,1,0:T(8,128)}) custom-call(s32[1,1024,1024]{2,1,0:T(8,128)} %codes.1, f32[32]{0:T(128)} %table.3, s32[2,2]{1,0:T(2,128)} %anchors.1), custom_call_target="tpu_custom_call" | custom-call | tf_op jit(solution)/shard_map/windows/pallas_call | solution.py:119
  6.3 13.5 %exchange.1 = (bf16[4,512,512]{2,1,0:T(8,128)(2,1)}, f32[4,8,128]{2,1,0:T(8,128)}) custom-call(bf16[2,512,512]{2,1,0:T(8,128)(2,1)} %get-tuple-element.9.win, f32[2,8,128]{2,1,0:T(8,128)} %get-tuple-element.10.means), custom_call_target="tpu_custom_call" | custom-call | tf_op jit(solution)/shard_map/exchange/pallas_call | solution.py:208
  19.8 41.2 %fields.1 = bf16[2,2,2,4,512,128]{5,4,3,2,1,0:T(8,128)(2,1)} custom-call(bf16[2,1,2,512,512]{4,3,2,1,0:T(8,128)(2,1)} %src.1, bf16[2,1,2,512,512]{4,3,2,1,0:T(8,128)(2,1)} %rec.1, bf16[4,512,512]{2,1,0:T(8,128)(2,1)} %get-tuple-element.11.codes, f32[4,8,128]{2,1,0:T(8,128)} %get-tuple-element.12.sums, f32[32]{0:T(128)} %table.3, ...), custom_call_target="tpu_custom_call" | custom-call | tf_op jit(solution)/shard_map/fields/pallas_call | solution.py:395
  61.0 59.1 %image.1 = f32[15,16,512]{2,1,0:T(8,128)} custom-call(bf16[2,2,2,4,512,128]{5,4,3,2,1,0:T(8,128)(2,1)} %fields.1), custom_call_target="tpu_custom_call" | custom-call | tf_op jit(solution)/shard_map/image/pallas_call | solution.py:602
  120.2 1.9 %copy.9 = f32[1,15,16,512]{3,2,1,0:T(8,128)} copy(f32[1,15,16,512]{3,2,1,0:T(8,128)} %bitcast.1) | data formatting | bytes 983040

commit v5 on v4

v5 whole, which is shorter than its diff:
```python
import functools
import math

import jax
import jax.numpy as jnp
import numpy as np
from jax import lax
from jax.experimental import pallas as pl
from jax.experimental.pallas import tpu as pltpu
from jax.sharding import PartitionSpec as P

LAG = 7
LAGS = 2 * LAG + 1
N = 512
B = 128
GROUPS = 5
PER = LAGS // GROUPS
MESH = pl.DeviceIdType.MESH
F32 = jnp.float32
BF16 = jnp.bfloat16


def butterfly_matrices():
    j = np.arange(B)[:, None]
    k = np.arange(B)[None, :]
    mats = []
    for wave in (4 * k, 4 * k + 1, 4 * k + 2, -(4 * k + 1)):
        angle = 2.0 * np.pi * ((j * wave) % N) / N
        c = np.cos(angle) / math.sqrt(N)
        s = np.sin(angle) / math.sqrt(N)
        mats.append(np.block([[c, -s], [s, c]]))
    right = np.stack(mats)
    return right, np.swapaxes(right, 1, 2)


def even_poly(first, terms, top, samples=400):
    q = (np.cos(np.pi * (np.arange(samples) + 0.5) / samples) + 1.0) * 0.5 * top
    r = np.sqrt(q)
    want = np.cos(r) if first == 0 else np.sin(r) / r
    fit = np.polynomial.Chebyshev.fit(q, want, terms, domain=[0, top])
    return [float(v) for v in fit.convert(kind=np.polynomial.Polynomial).coef]


COS_Q = even_poly(0, 6, 14.0)
SIN_Q = even_poly(1, 6, 14.0)


def horner(coefs, q):
    value = coefs[-1] * q + coefs[-2]
    for c in coefs[-3::-1]:
        value = value * q + c
    return value


def split4(re, im):
    er, ei, dr, di = re[0] + re[2], im[0] + im[2], re[0] - re[2], im[0] - im[2]
    fr, fi, gr, gi = re[1] + re[3], im[1] + im[3], re[1] - re[3], im[1] - im[3]
    return (er + fr, dr + gi, er - fr, dr - gi), (ei + fi, di - gr, ei - fi, di + gr)


def join4(re, im):
    er, ei, dr, di = re[0] + re[2], im[0] + im[2], re[0] - re[2], im[0] - im[2]
    fr, fi, gr, gi = re[1] + re[3], im[1] + im[3], re[1] - re[3], im[1] - im[3]
    return (er + fr, dr - gi, er - fr, dr + gi), (ei + fi, di + gr, ei - fi, di - gr)


def level_row(table):
    lane = lax.broadcasted_iota(jnp.int32, (8, B), 1)
    levels = jnp.zeros((8, B), F32)
    for k in range(32):
        levels = jnp.where(lane == k, table[k], levels)
    return levels


TAKE = lax.GatherDimensionNumbers(
    offset_dims=(), collapsed_slice_dims=(1,), start_index_map=(1,),
    operand_batching_dims=(0,), start_indices_batching_dims=(0,))


def lookup(values, index):
    return lax.gather(
        jnp.tile(values, (index.shape[0] // 8, 1)), index[..., None], TAKE, (1, 1),
        mode=lax.GatherScatterMode.PROMISE_IN_BOUNDS)


def windows_kernel(codes, table, anchors, out, means, raw, sem):
    def fetch(s, h):
        ox = pl.multiple_of(anchors[s, 0], N)
        oy = pl.multiple_of(anchors[s, 1], N)
        return pltpu.make_async_copy(
            codes.at[0, pl.ds(ox + h * 256, 256), pl.ds(oy, N)], raw.at[s, h], sem.at[s, h])

    for s in range(2):
        for h in range(2):
            fetch(s, h).start()
    levels = level_row(table)
    for s in range(2):
        total = jnp.zeros((8, B), F32)
        for h in range(2):
            fetch(s, h).wait()

            def rows_of(n, total):
                take = pl.ds(pl.multiple_of(n * 32, 32), 32)
                for q in range(4):
                    index = raw[s, h, take, q * B:(q + 1) * B]
                    out[s, pl.ds(pl.multiple_of(h * 256 + n * 32, 32), 32), q * B:(q + 1) * B] = (
                        index.astype(F32).astype(BF16))
                    got = lookup(levels, index)
                    total = total + (got[0:8] + got[8:16]) + (got[16:24] + got[24:32])
                return total

            total = lax.fori_loop(0, 8, rows_of, total)
        means[s] = jnp.full((8, B), jnp.sum(total) * (1.0 / (N * N)), F32)


def make_windows(codes, table, anchors):
    vmem = pl.BlockSpec(memory_space=pltpu.VMEM)
    smem = pl.BlockSpec(memory_space=pltpu.SMEM)
    return pl.pallas_call(
        windows_kernel,
        out_shape=(
            jax.ShapeDtypeStruct((2, N, N), BF16),
            jax.ShapeDtypeStruct((2, 8, B), F32),
        ),
        in_specs=[pl.BlockSpec(memory_space=pl.ANY), smem, smem],
        out_specs=(vmem, vmem),
        scratch_shapes=[pltpu.VMEM((2, 2, 256, N), jnp.int32), pltpu.SemaphoreType.DMA((2, 2))],
        compiler_params=pltpu.CompilerParams(vmem_limit_bytes=60 * 1024 * 1024),
        name="windows",
    )(codes, table, anchors)


def migrate_kernel(
    factor, src, rec, win, means, table, right_ref, left_ref, out,
    u, a, cbuf, mbuf, ph, sc, raw, pad, buf, r1, r2, r3, fa, fb,
    tsem, csend, crecv, msend, mrecv, esend, erecv, ssem, rsem, fsend, frecv,
):
    depth = lax.axis_index("depth")
    freq = lax.axis_index("freq")
    core = depth % 2
    section = depth // 2
    other = depth + 1 - 2 * core
    x, z, yh = freq % 4, (freq // 4) % 4, freq // 16
    first_plane = section * 2
    steps = first_plane + 2
    ring = (
        freq - x + (x + 1 - 2 * (x % 2)),
        freq - x + (3 - x),
        freq - 4 * z + 4 * (z + 1 - 2 * (z % 2)),
        freq - 4 * z + 4 * (3 - z),
    )
    far = freq - 16 * yh + 16 * (1 - yh)
    far_ring = [r - 16 * yh + 16 * (1 - yh) for r in ring]
    sibling = (other, freq)
    beside = [[(2 * (1 - section) + s, freq) for s in range(2)], [(2 * (1 - section) + s, far) for s in range(2)]]

    def bits(ix, iz):
        return [((ix + 1) // 2) % 2, ix // 2, ((iz + 1) // 2) % 2, iz // 2]

    mine = bits(x, z)
    side = mine

    tops = []
    for kind, top in enumerate((src, rec)):
        for q in range(4):
            tops.append(pltpu.make_async_copy(
                top.at[core, 0, :, :, pl.ds(q * B, B)], u.at[2, kind, :, q], tsem.at[kind, q]))
    for copy_in in tops:
        copy_in.start()

    def half_rows(way):
        return pl.ds(way * (N // 2), N // 2)

    for way in range(2):
        pltpu.make_async_copy(
            win.at[core, half_rows(way)], cbuf.at[depth, half_rows(way)], crecv.at[depth, way]).start()
    mbuf[depth] = means[core]

    barrier = pltpu.get_barrier_semaphore()
    peers = [sibling, (depth, far)] + beside[0] + beside[1]
    for i in range(4):
        peers += [(depth, ring[i]), (other, ring[i]), (depth, far_ring[i])]
    for who in peers:
        pl.semaphore_signal(barrier, inc=1, device_id=who, device_id_type=MESH)

    position = freq.astype(F32)
    angular = math.pi * (0.45 + 0.5 * (position + 0.5) / 32.0)
    levels = level_row(table)
    angle = angular * levels
    squared = angle * angle
    cos_levels = horner(COS_Q, squared)
    sin_levels = angle * horner(SIN_Q, squared)
    pl.semaphore_wait(barrier, len(peers))

    def codes_to(n, way, who):
        shot = (0, 1, 1 - core)[n]
        return pltpu.make_async_remote_copy(
            src_ref=win.at[shot, half_rows(way)], dst_ref=cbuf.at[depth, half_rows(way)],
            send_sem=csend.at[n, way], recv_sem=crecv.at[depth, way],
            device_id=who, device_id_type=MESH)

    def mean_to(n, who):
        shot = (0, 1, 1 - core)[n]
        return pltpu.make_async_remote_copy(
            src_ref=means.at[shot], dst_ref=mbuf.at[depth],
            send_sem=msend.at[n], recv_sem=mrecv.at[depth],
            device_id=who, device_id_type=MESH)

    def section_codes(act):
        for s in range(2):
            for way in range(2):
                act(codes_to(s, way, beside[way][s]))

    mean_to(2, sibling).start()

    @pl.when(section == 0)
    def _():
        for s in range(2):
            mean_to(s, beside[0][s]).start()

    for way in range(2):
        codes_to(2, way, sibling).start()

    @pl.when(jnp.logical_and(section == 0, core == 0))
    def _():
        section_codes(lambda c: c.start())

    def window(i, half):
        return pl.ds(pl.multiple_of(half * 240, 16), 272)

    def hand(i, n):
        plane = (1 - core, core, 1 - core)[n]
        half = (side[i], 1 - side[i], 1 - side[i])[n]
        who = (sibling, (depth, ring[i]), (other, ring[i]))[n]
        return pltpu.make_async_remote_copy(
            src_ref=u.at[plane, :, :, i, window(i, half)], dst_ref=raw.at[i, n],
            send_sem=esend.at[i, n], recv_sem=erecv.at[i, n],
            device_id=who, device_id_type=MESH)

    def hand_plane(q):
        @pl.when(core == q)
        def _():
            for i in range(4):
                hand(i, 1).start()

        @pl.when(core != q)
        def _():
            for n in (2, 0):
                for i in range(4):
                    hand(i, n).start()

    for copy_in in tops:
        copy_in.wait()

    def step(plane, carry):
        z = plane
        new = jnp.where(z < first_plane, 2, z - first_plane)
        old = jnp.where(z <= first_plane, 2, z - 1 - first_plane)

        def wide(ref, kind, p, half, block):
            rows = slice(block * B, (block + 1) * B)
            return jnp.concatenate([ref[kind, p, half * 2, rows, :], ref[kind, p, half * 2 + 1, rows, :]], axis=1)

        def put_wide(ref, kind, p, half, block, value):
            rows = slice(block * B, (block + 1) * B)
            ref[kind, p, half * 2, rows, :] = value[:, :B]
            ref[kind, p, half * 2 + 1, rows, :] = value[:, B:]

        def wide_u(kind, p, half, block):
            rows = slice(block * B, (block + 1) * B)
            return jnp.concatenate([u[old, kind, p, half * 2, rows, :], u[old, kind, p, half * 2 + 1, rows, :]], axis=1)

        def forward_x(n, carry):
            kind, half = n % 2, n // 2
            re = [wide_u(kind, 0, half, q) for q in range(4)]
            im = [wide_u(kind, 1, half, q) for q in range(4)]
            sre, sim = split4(re, im)
            for r in range(4):
                got = jnp.dot(left_ref[r], jnp.concatenate([sre[r], sim[r]], axis=0),
                              preferred_element_type=F32).astype(BF16)
                put_wide(a, kind, 0, half, r, got[:B])
                put_wide(a, kind, 1, half, r, got[B:])
            return carry

        lax.fori_loop(0, 4, forward_x, 0, unroll=2)

        @pl.when(z == first_plane + 1)
        def _():
            hand_plane(0)

        for way in range(2):
            pltpu.make_async_copy(
                win.at[0, half_rows(way)], cbuf.at[z, half_rows(way)], crecv.at[z, way]).wait()

        @pl.when(z != depth)
        def _():
            pltpu.make_async_copy(means.at[0], mbuf.at[z], mrecv.at[z]).wait()

        base = mbuf[z, 0:1, :]
        turn = angular * base
        turn_sq = turn * turn
        turn_re = horner(COS_Q, turn_sq)
        turn_im = turn * horner(SIN_Q, turn_sq)

        def operators(n, carry):
            rows = n * 24
            k = rows + lax.broadcasted_iota(jnp.int32, (24, B), 0)
            kx = (k % B) * 4 + k // B
            kx = jnp.where(kx < N // 2, kx, kx - N).astype(F32) * (2.0 * math.pi / N)
            left_q = turn_sq - kx * kx
            for ry in range(3):
                ky = lax.broadcasted_iota(jnp.int32, (1, B), 1) * 4 + ry
                ky = jnp.where(ky < N // 2, ky, ky - N).astype(F32) * (2.0 * math.pi / N)
                q = left_q - ky * ky
                root = jnp.sqrt(jnp.abs(q))
                wave = jnp.maximum(q, 0.0)
                travels = q >= 0.0
                pre = jnp.where(travels, horner(COS_Q, wave), jnp.exp(-root))
                pim = jnp.where(travels, root * horner(SIN_Q, wave), 0.0)
                put = pl.ds(pl.multiple_of(rows, 8), 24)
                ph[0, ry, put, :] = pre * turn_re + pim * turn_im
                ph[1, ry, put, :] = pim * turn_re - pre * turn_im
            take = pl.ds(pl.multiple_of(n * 32, 32), 32)
            for q in range(4):
                index = cbuf[z, take, q * B:(q + 1) * B].astype(jnp.int32)
                sc[0, q, take, :] = lookup(cos_levels, index)
                sc[1, q, take, :] = lookup(sin_levels, index)
            return carry

        lax.fori_loop(0, 16, operators, 0, unroll=2)

        def along_y(rx, carry):
            prow = pl.ds(pl.multiple_of(jnp.where(rx == 3, 1, rx) * B, B), B)
            rows = pl.ds(pl.multiple_of(rx * B, B), B)
            sums_of = [split4([a[k, 0, q, rows, :] for q in range(4)], [a[k, 1, q, rows, :] for q in range(4)])
                       for k in range(2)]
            tre, tim = ([], []), ([], [])
            for r in range(4):
                data = jnp.concatenate(
                    [jnp.concatenate([sums_of[k][0][r], sums_of[k][1][r]], axis=1) for k in range(2)], axis=0)
                got = jnp.dot(data, right_ref[r], preferred_element_type=F32)
                py = 1 if r == 3 else r
                pre, pim = ph[0, py, prow, :], ph[1, py, prow, :]
                turned = []
                for k in range(2):
                    gre, gim = got[k * B:(k + 1) * B, :B], got[k * B:(k + 1) * B, B:]
                    rr, ii, ri, ir = gre * pre, gim * pim, gre * pim, gim * pre
                    nre, nim = (rr - ii, ri + ir) if k == 0 else (rr + ii, ir - ri)
                    turned.append(jnp.concatenate([nre.astype(BF16), nim.astype(BF16)], axis=1))
                back = jnp.dot(jnp.concatenate(turned, axis=0), left_ref[r], preferred_element_type=F32)
                for k in range(2):
                    tre[k].append(back[k * B:(k + 1) * B, :B])
                    tim[k].append(back[k * B:(k + 1) * B, B:])
            for k in range(2):
                cre, cim = join4(tre[k], tim[k])
                for q in range(4):
                    a[k, 0, q, rows, :] = cre[q].astype(BF16)
                    a[k, 1, q, rows, :] = cim[q].astype(BF16)
            return carry

        lax.fori_loop(0, 4, along_y, 0)

        @pl.when(jnp.logical_and(z == 0, jnp.logical_and(section == 0, core == 1)))
        def _():
            section_codes(lambda c: c.start())

        def inverse_x(n, carry):
            kind, half = n % 2, n // 2
            sign = (1 - 2 * kind).astype(F32)
            tre, tim = [], []
            for r in range(4):
                data = jnp.concatenate([wide(a, kind, 0, half, r), wide(a, kind, 1, half, r)], axis=0)
                got = jnp.dot(right_ref[r], data, preferred_element_type=F32)
                tre.append(got[:B])
                tim.append(got[B:])
            xre, xim = join4(tre, tim)
            for q in range(4):
                rows = slice(q * B, (q + 1) * B)
                for part in range(2):
                    cols = slice(part * B, (part + 1) * B)
                    cre = sc[0, half * 2 + part, rows, :]
                    cim = sc[1, half * 2 + part, rows, :] * sign
                    gre, gim = xre[q][:, cols], xim[q][:, cols]
                    u[new, kind, 0, half * 2 + part, rows, :] = (gre * cre - gim * cim).astype(BF16)
                    u[new, kind, 1, half * 2 + part, rows, :] = (gre * cim + gim * cre).astype(BF16)
            return carry

        lax.fori_loop(0, 4, inverse_x, 0, unroll=2)

        return carry

    lax.fori_loop(0, steps, step, 0)

    for i in range(4):
        for s in range(4):
            for k in range(2):
                for p in range(2):
                    pad[i, s, k, p, 0:8, :] = jnp.zeros((8, B), F32)
                    pad[i, s, k, p, 280:288, :] = jnp.zeros((8, B), F32)
    hand_plane(1)

    for i in range(4):
        for k in range(2):
            for p in range(2):
                pad[i, 0, k, p, 8:280, :] = u[core, k, p, i, window(i, side[i]), :].astype(F32)
    for n in range(3):
        for i in range(4):
            hand(i, n).wait_recv()
            for k in range(2):
                for p in range(2):
                    pad[i, n + 1, k, p, 8:280, :] = raw[i, n, k, p].astype(F32)

    def weight(d, i):
        return (1, 8, 4, 2)[(d - i) % 4]

    flip_x = [[(mine[d] + bits(v, 0)[d]) % 2 for d in range(2)] for v in range(4)]
    slot_x = [[sum(flip_x[v][d] * weight(d, i) for d in range(2)) for i in range(4)] for v in range(4)]
    shift = [side[i] * 16 for i in range(4)]

    def produce(g):
        def body(n, carry):
            theirs = bits(0, n)
            flip_z = [(mine[d] + theirs[d]) % 2 for d in (2, 3)]
            slot_z = [sum(flip_z[d - 2] * weight(d, i) for d in (2, 3)) for i in range(4)]
            for v in range(4):
                for i in range(4):
                    row = pl.multiple_of(n * 64 + v * 16 + shift[i], 16)
                    slot = slot_z[i] + slot_x[v][i]
                    for l in range(PER):
                        h = g * PER + l - LAG
                        total = None
                        for s in range(4):
                            for p in range(2):
                                left = pad[i, s, 0, p, pl.ds(row + (8 - h), 16), :]
                                right = pad[i, s, 1, p, pl.ds(row + (8 + h), 16), :]
                                term = left * right
                                total = term if total is None else total + term
                        buf[g, i, slot, l] = total.astype(BF16)
            return carry
        lax.fori_loop(0, 4, body, 0)

    recv = (None, r1, r2, r3)

    def copy(g, i, t):
        half = 16 >> t
        return pltpu.make_async_remote_copy(
            src_ref=buf.at[g, i, pl.ds(half, half)], dst_ref=recv[t].at[g, i],
            send_sem=ssem.at[g, i, t - 1], recv_sem=rsem.at[g, i, t - 1],
            device_id=(depth, ring[(i + t) % 4]), device_id_type=MESH)

    def last(i, slot, who, place):
        return pltpu.make_async_remote_copy(
            src_ref=buf.at[:, i, slot], dst_ref=(fa, fb)[place].at[i],
            send_sem=fsend.at[i, slot], recv_sem=frecv.at[i, place],
            device_id=who, device_id_type=MESH)

    at_home = [side[i] == yh for i in range(4)]

    def sends_last(i, act):
        @pl.when(at_home[i])
        def _():
            act(last(i, 1, (depth, ring[i]), 0))

        @pl.when(jnp.logical_not(at_home[i]))
        def _():
            act(last(i, 0, (depth, far), 0))
            act(last(i, 1, (depth, far_ring[i]), 1))

    def arrive(g, i, t):
        copy(g, i, t).wait_recv()
        half = 16 >> t

        def body(n, carry):
            for k in (half - 1 - 2 * n, half - 2 - 2 * n):
                buf[g, i, k] = buf[g, i, k] + recv[t][g, i, k]
            return carry
        lax.fori_loop(0, half // 2, body, 0)
        if t < 3:
            copy(g, i, t + 1).start()

    def finish(i):
        last(i, 0, (depth, far), 0).wait_recv()
        cols = slice(i * B, (i + 1) * B)

        @pl.when(at_home[i])
        def _():
            for g in range(GROUPS):
                out[g * PER:(g + 1) * PER, :, cols] = (buf[g, i, 0].astype(F32) + fa[i, g].astype(F32)) * factor

        @pl.when(jnp.logical_not(at_home[i]))
        def _():
            last(i, 1, (depth, far_ring[i]), 1).wait_recv()
            for g in range(GROUPS):
                out[g * PER:(g + 1) * PER, :, cols] = (fa[i, g].astype(F32) + fb[i, g].astype(F32)) * factor

    for g in range(GROUPS):
        produce(g)
        for i in range(4):
            copy(g, i, 1).start()
        if g >= 2:
            for i in range(4):
                arrive(g - 2, i, 1)
    for g in range(GROUPS - 2, GROUPS):
        for i in range(4):
            arrive(g, i, 1)
    for t in (2, 3):
        for g in range(GROUPS):
            for i in range(4):
                arrive(g, i, t)
                if t == 3 and g == GROUPS - 1:
                    sends_last(i, lambda c: c.start())
    for i in range(4):
        finish(i)
    for i in range(4):
        for n in range(3):
            hand(i, n).wait_send()
    for g in range(GROUPS):
        for i in range(4):
            for t in (1, 2, 3):
                copy(g, i, t).wait_send()
    for i in range(4):
        sends_last(i, lambda c: c.wait_send())
    for way in range(2):
        codes_to(2, way, sibling).wait_send()
    mean_to(2, sibling).wait_send()

    @pl.when(section == 0)
    def _():
        section_codes(lambda c: c.wait_send())
        for s in range(2):
            mean_to(s, beside[0][s]).wait_send()


def migrate(src, rec, win, means, table, right, left, factor):
    vmem = pl.BlockSpec(memory_space=pltpu.VMEM)
    hbm = pl.BlockSpec(memory_space=pl.ANY)
    dma = pltpu.SemaphoreType.DMA
    strip = (PER, 16, B)
    return pl.pallas_call(
        functools.partial(migrate_kernel, factor),
        out_shape=jax.ShapeDtypeStruct((LAGS, 16, N), F32),
        in_specs=[hbm, hbm, hbm, vmem, pl.BlockSpec(memory_space=pltpu.SMEM), vmem, vmem],
        out_specs=vmem,
        scratch_shapes=[
            pltpu.VMEM((3, 2, 2, 4, N, B), BF16),
            pltpu.VMEM((2, 2, 4, N, B), BF16),
            pltpu.VMEM((4, N, N), BF16),
            pltpu.VMEM((4, 8, B), F32),
            pltpu.VMEM((2, 3, 3 * B, B), F32),
            pltpu.VMEM((2, 4, N, B), F32),
            pltpu.VMEM((4, 3, 2, 2, 272, B), BF16),
            pltpu.VMEM((4, 4, 2, 2, 288, B), F32),
            pltpu.VMEM((GROUPS, 4, 16) + strip, BF16),
            pltpu.VMEM((GROUPS, 4, 8) + strip, BF16),
            pltpu.VMEM((GROUPS, 4, 4) + strip, BF16),
            pltpu.VMEM((GROUPS, 4, 2) + strip, BF16),
            pltpu.VMEM((4, GROUPS) + strip, BF16),
            pltpu.VMEM((4, GROUPS) + strip, BF16),
            dma((2, 4)), dma((3, 2)), dma((4, 2)), dma((3,)), dma((4,)),
            dma((4, 3)), dma((4, 3)),
            dma((GROUPS, 4, 3)), dma((GROUPS, 4, 3)), dma((4, 2)), dma((4, 2)),
        ],
        compiler_params=pltpu.CompilerParams(
            collective_id=1, has_side_effects=True, vmem_limit_bytes=62 * 1024 * 1024),
        name="migrate",
    )(src, rec, win, means, table, right, left)


def shards(source_top, receiver_top, slowness_codes, slowness_table, anchors):
    right, left = butterfly_matrices()
    right = jnp.asarray(right, BF16)
    left = jnp.asarray(left, BF16)
    windows, means = make_windows(slowness_codes, slowness_table, anchors)
    image = migrate(
        source_top, receiver_top, windows, means, slowness_table, right, left, 1.0 / math.sqrt(128.0))
    return image[None]


def solution(mesh):
    return jax.shard_map(
        shards,
        mesh=mesh,
        in_specs=(
            P(None, "freq", None, None, None),
            P(None, "freq", None, None, None),
            P("depth", None, None),
            P(),
            P(),
        ),
        out_specs=P("depth", None, "freq", None),
        check_vma=False,
    )
```

time: 122 us -> 91.1 us (0.75)
  the two profiles are of different devices: /device:TPU:8 before, /device:TPU:9 now
where the time goes in v5:
time: 91.1 us; the launch traced here: 90.9 us
  Pallas kernels  89 us (98%)
  local copies, waits for them, and re-layouts  1.85 us (2%)
    pallas_call x1, Pallas kernels, migrate(): pl.pallas_call(functools.partial(migrate_kernel, factor), out_shape=jax.S...  82.7 us
    pallas_call x1, Pallas kernels, make_windows(): pl.pallas_call(windows_kernel, out_shape=(jax.ShapeDtypeStruct((2, N, N),...  6.32 us
    unnamed x1, local copies, waits for them, and re-layouts  1.85 us

profile of v5, /device:TPU:9, one launch (start us, length us, event | category | flops | bytes accessed | tf_op | source)
XLA Modules:
  0.0 90.9 jit_solution(10977836344090769670)
XLA Ops:
  0.0 6.3 %windows.1 = (bf16[2,512,512]{2,1,0:T(8,128)(2,1)}, f32[2,8,128]{2,1,0:T(8,128)}) custom-call(s32[1,1024,1024]{2,1,0:T(8,128)} %codes.1, f32[32]{0:T(128)} %table.3, s32[2,2]{1,0:T(2,128)} %anchors.1), custom_call_target="tpu_custom_call" | custom-call | tf_op jit(solution)/shard_map/windows/pallas_call | solution.py:119
  6.3 82.7 %migrate.1 = f32[15,16,512]{2,1,0:T(8,128)} custom-call(bf16[2,1,2,512,512]{4,3,2,1,0:T(8,128)(2,1)} %src.1, bf16[2,1,2,512,512]{4,3,2,1,0:T(8,128)(2,1)} %rec.1, bf16[2,512,512]{2,1,0:T(8,128)(2,1)} %get-tuple-element.7.win, f32[2,8,128]{2,1,0:T(8,128)} %get-tuple-element.8.means, f32[32]{0:T(128)} %table.3, bf16[4,256,256]{2,1,0:T(8,128)(2,1)} %constant.4.clone.right_ref, ...), custom_call_target="tpu_custom_call" | custom-call | tf_op jit(solution)/shard_map/migrate/pallas_call | solution.py:539
  89.0 1.9 %copy.9 = f32[1,15,16,512]{3,2,1,0:T(8,128)} copy(f32[1,15,16,512]{3,2,1,0:T(8,128)} %bitcast.1) | data formatting | bytes 983040

commit v6 on v5

--- a/solution.py
+++ b/solution.py
@@ -42,7 +42,7 @@
 
 
 COS_Q = even_poly(0, 6, 14.0)
-SIN_Q = even_poly(1, 6, 14.0)
+SIN_Q = even_poly(1, 5, 14.0)
 
 
 def horner(coefs, q):
@@ -186,10 +186,6 @@
     position = freq.astype(F32)
     angular = math.pi * (0.45 + 0.5 * (position + 0.5) / 32.0)
     levels = level_row(table)
-    angle = angular * levels
-    squared = angle * angle
-    cos_levels = horner(COS_Q, squared)
-    sin_levels = angle * horner(SIN_Q, squared)
     pl.semaphore_wait(barrier, len(peers))
 
     def codes_to(n, way, who):
@@ -282,7 +278,7 @@
                 put_wide(a, kind, 1, half, r, got[B:])
             return carry
 
-        lax.fori_loop(0, 4, forward_x, 0, unroll=2)
+        lax.fori_loop(0, 4, forward_x, 0, unroll=4)
 
         @pl.when(z == first_plane + 1)
         def _():
@@ -299,12 +295,14 @@
         base = mbuf[z, 0:1, :]
         turn = angular * base
         turn_sq = turn * turn
-        turn_re = horner(COS_Q, turn_sq)
-        turn_im = turn * horner(SIN_Q, turn_sq)
+        angle = angular * (levels - base)
+        squared = angle * angle
+        cos_levels = horner(COS_Q, squared)
+        sin_levels = angle * horner(SIN_Q, squared)
 
         def operators(n, carry):
-            rows = n * 24
-            k = rows + lax.broadcasted_iota(jnp.int32, (24, B), 0)
+            rows = n * 48
+            k = rows + lax.broadcasted_iota(jnp.int32, (48, B), 0)
             kx = (k % B) * 4 + k // B
             kx = jnp.where(kx < N // 2, kx, kx - N).astype(F32) * (2.0 * math.pi / N)
             left_q = turn_sq - kx * kx
@@ -312,22 +310,20 @@
                 ky = lax.broadcasted_iota(jnp.int32, (1, B), 1) * 4 + ry
                 ky = jnp.where(ky < N // 2, ky, ky - N).astype(F32) * (2.0 * math.pi / N)
                 q = left_q - ky * ky
-                root = jnp.sqrt(jnp.abs(q))
-                wave = jnp.maximum(q, 0.0)
+                size = jnp.maximum(jnp.abs(q), 1e-30)
+                root = size * lax.rsqrt(size)
                 travels = q >= 0.0
-                pre = jnp.where(travels, horner(COS_Q, wave), jnp.exp(-root))
-                pim = jnp.where(travels, root * horner(SIN_Q, wave), 0.0)
-                put = pl.ds(pl.multiple_of(rows, 8), 24)
-                ph[0, ry, put, :] = pre * turn_re + pim * turn_im
-                ph[1, ry, put, :] = pim * turn_re - pre * turn_im
-            take = pl.ds(pl.multiple_of(n * 32, 32), 32)
+                put = pl.ds(pl.multiple_of(rows, 16), 48)
+                ph[0, ry, put, :] = jnp.where(travels, horner(COS_Q, q), jnp.exp(-root)).astype(BF16)
+                ph[1, ry, put, :] = jnp.where(travels, root * horner(SIN_Q, q), 0.0).astype(BF16)
+            take = pl.ds(pl.multiple_of(n * 64, 64), 64)
             for q in range(4):
                 index = cbuf[z, take, q * B:(q + 1) * B].astype(jnp.int32)
-                sc[0, q, take, :] = lookup(cos_levels, index)
-                sc[1, q, take, :] = lookup(sin_levels, index)
+                sc[0, q, take, :] = lookup(cos_levels, index).astype(BF16)
+                sc[1, q, take, :] = lookup(sin_levels, index).astype(BF16)
             return carry
 
-        lax.fori_loop(0, 16, operators, 0, unroll=2)
+        lax.fori_loop(0, 8, operators, 0)
 
         def along_y(rx, carry):
             prow = pl.ds(pl.multiple_of(jnp.where(rx == 3, 1, rx) * B, B), B)
@@ -338,7 +334,7 @@
             for r in range(4):
                 data = jnp.concatenate(
                     [jnp.concatenate([sums_of[k][0][r], sums_of[k][1][r]], axis=1) for k in range(2)], axis=0)
-                got = jnp.dot(data, right_ref[r], preferred_element_type=F32)
+                got = jnp.dot(data, right_ref[r], preferred_element_type=F32).astype(BF16)
                 py = 1 if r == 3 else r
                 pre, pim = ph[0, py, prow, :], ph[1, py, prow, :]
                 turned = []
@@ -346,19 +342,19 @@
                     gre, gim = got[k * B:(k + 1) * B, :B], got[k * B:(k + 1) * B, B:]
                     rr, ii, ri, ir = gre * pre, gim * pim, gre * pim, gim * pre
                     nre, nim = (rr - ii, ri + ir) if k == 0 else (rr + ii, ir - ri)
-                    turned.append(jnp.concatenate([nre.astype(BF16), nim.astype(BF16)], axis=1))
-                back = jnp.dot(jnp.concatenate(turned, axis=0), left_ref[r], preferred_element_type=F32)
+                    turned.append(jnp.concatenate([nre, nim], axis=1))
+                back = jnp.dot(jnp.concatenate(turned, axis=0), left_ref[r], preferred_element_type=F32).astype(BF16)
                 for k in range(2):
                     tre[k].append(back[k * B:(k + 1) * B, :B])
                     tim[k].append(back[k * B:(k + 1) * B, B:])
             for k in range(2):
                 cre, cim = join4(tre[k], tim[k])
                 for q in range(4):
-                    a[k, 0, q, rows, :] = cre[q].astype(BF16)
-                    a[k, 1, q, rows, :] = cim[q].astype(BF16)
+                    a[k, 0, q, rows, :] = cre[q]
+                    a[k, 1, q, rows, :] = cim[q]
             return carry
 
-        lax.fori_loop(0, 4, along_y, 0)
+        lax.fori_loop(0, 4, along_y, 0, unroll=4)
 
         @pl.when(jnp.logical_and(z == 0, jnp.logical_and(section == 0, core == 1)))
         def _():
@@ -366,11 +362,11 @@
 
         def inverse_x(n, carry):
             kind, half = n % 2, n // 2
-            sign = (1 - 2 * kind).astype(F32)
+            sign = (1 - 2 * kind).astype(F32).astype(BF16)
             tre, tim = [], []
             for r in range(4):
                 data = jnp.concatenate([wide(a, kind, 0, half, r), wide(a, kind, 1, half, r)], axis=0)
-                got = jnp.dot(right_ref[r], data, preferred_element_type=F32)
+                got = jnp.dot(right_ref[r], data, preferred_element_type=F32).astype(BF16)
                 tre.append(got[:B])
                 tim.append(got[B:])
             xre, xim = join4(tre, tim)
@@ -381,11 +377,11 @@
                     cre = sc[0, half * 2 + part, rows, :]
                     cim = sc[1, half * 2 + part, rows, :] * sign
                     gre, gim = xre[q][:, cols], xim[q][:, cols]
-                    u[new, kind, 0, half * 2 + part, rows, :] = (gre * cre - gim * cim).astype(BF16)
-                    u[new, kind, 1, half * 2 + part, rows, :] = (gre * cim + gim * cre).astype(BF16)
+                    u[new, kind, 0, half * 2 + part, rows, :] = gre * cre - gim * cim
+                    u[new, kind, 1, half * 2 + part, rows, :] = gre * cim + gim * cre
             return carry
 
-        lax.fori_loop(0, 4, inverse_x, 0, unroll=2)
+        lax.fori_loop(0, 4, inverse_x, 0, unroll=4)
 
         return carry
 
@@ -448,23 +444,23 @@
             send_sem=ssem.at[g, i, t - 1], recv_sem=rsem.at[g, i, t - 1],
             device_id=(depth, ring[(i + t) % 4]), device_id_type=MESH)
 
-    def last(i, slot, who, place):
+    def last(g, i, slot, who, place):
         return pltpu.make_async_remote_copy(
-            src_ref=buf.at[:, i, slot], dst_ref=(fa, fb)[place].at[i],
-            send_sem=fsend.at[i, slot], recv_sem=frecv.at[i, place],
+            src_ref=buf.at[g, i, slot], dst_ref=(fa, fb)[place].at[g, i],
+            send_sem=fsend.at[g, i, slot], recv_sem=frecv.at[g, i, place],
             device_id=who, device_id_type=MESH)
 
     at_home = [side[i] == yh for i in range(4)]
 
-    def sends_last(i, act):
+    def sends_last(g, i, act):
         @pl.when(at_home[i])
         def _():
-            act(last(i, 1, (depth, ring[i]), 0))
+            act(last(g, i, 1, (depth, ring[i]), 0))
 
         @pl.when(jnp.logical_not(at_home[i]))
         def _():
-            act(last(i, 0, (depth, far), 0))
-            act(last(i, 1, (depth, far_ring[i]), 1))
+            act(last(g, i, 0, (depth, far), 0))
+            act(last(g, i, 1, (depth, far_ring[i]), 1))
 
     def arrive(g, i, t):
         copy(g, i, t).wait_recv()
@@ -477,40 +473,37 @@
         lax.fori_loop(0, half // 2, body, 0)
         if t < 3:
             copy(g, i, t + 1).start()
-
-    def finish(i):
-        last(i, 0, (depth, far), 0).wait_recv()
-        cols = slice(i * B, (i + 1) * B)
+        else:
+            sends_last(g, i, lambda c: c.start())
+
+    def finish(g, i):
+        last(g, i, 0, (depth, far), 0).wait_recv()
+        put = (slice(g * PER, (g + 1) * PER), slice(None), slice(i * B, (i + 1) * B))
 
         @pl.when(at_home[i])
         def _():
-            for g in range(GROUPS):
-                out[g * PER:(g + 1) * PER, :, cols] = (buf[g, i, 0].astype(F32) + fa[i, g].astype(F32)) * factor
+            out[put] = (buf[g, i, 0].astype(F32) + fa[g, i].astype(F32)) * factor
 
         @pl.when(jnp.logical_not(at_home[i]))
         def _():
-            last(i, 1, (depth, far_ring[i]), 1).wait_recv()
-            for g in range(GROUPS):
-                out[g * PER:(g + 1) * PER, :, cols] = (fa[i, g].astype(F32) + fb[i, g].astype(F32)) * factor
+            last(g, i, 1, (depth, far_ring[i]), 1).wait_recv()
+            out[put] = (fa[g, i].astype(F32) + fb[g, i].astype(F32)) * factor
 
     for g in range(GROUPS):
         produce(g)
         for i in range(4):
             copy(g, i, 1).start()
-        if g >= 2:
-            for i in range(4):
-                arrive(g - 2, i, 1)
-    for g in range(GROUPS - 2, GROUPS):
+        for t in (3, 2, 1):
+            if g - 1 - t >= 0:
+                for i in range(4):
+                    arrive(g - 1 - t, i, t)
+    left = [(g, t) for t in (1, 2, 3) for g in range(GROUPS) if g + t > GROUPS - 2]
+    for g, t in sorted(left, key=lambda gt: (gt[0] + gt[1], gt[1])):
         for i in range(4):
-            arrive(g, i, 1)
-    for t in (2, 3):
-        for g in range(GROUPS):
-            for i in range(4):
-                arrive(g, i, t)
-                if t == 3 and g == GROUPS - 1:
-                    sends_last(i, lambda c: c.start())
-    for i in range(4):
-        finish(i)
+            arrive(g, i, t)
+    for g in range(GROUPS):
+        for i in range(4):
+            finish(g, i)
     for i in range(4):
         for n in range(3):
             hand(i, n).wait_send()
@@ -518,8 +511,7 @@
         for i in range(4):
             for t in (1, 2, 3):
                 copy(g, i, t).wait_send()
-    for i in range(4):
-        sends_last(i, lambda c: c.wait_send())
+            sends_last(g, i, lambda c: c.wait_send())
     for way in range(2):
         codes_to(2, way, sibling).wait_send()
     mean_to(2, sibling).wait_send()
@@ -546,19 +538,19 @@
             pltpu.VMEM((2, 2, 4, N, B), BF16),
             pltpu.VMEM((4, N, N), BF16),
             pltpu.VMEM((4, 8, B), F32),
-            pltpu.VMEM((2, 3, 3 * B, B), F32),
-            pltpu.VMEM((2, 4, N, B), F32),
+            pltpu.VMEM((2, 3, 3 * B, B), BF16),
+            pltpu.VMEM((2, 4, N, B), BF16),
             pltpu.VMEM((4, 3, 2, 2, 272, B), BF16),
             pltpu.VMEM((4, 4, 2, 2, 288, B), F32),
             pltpu.VMEM((GROUPS, 4, 16) + strip, BF16),
             pltpu.VMEM((GROUPS, 4, 8) + strip, BF16),
             pltpu.VMEM((GROUPS, 4, 4) + strip, BF16),
             pltpu.VMEM((GROUPS, 4, 2) + strip, BF16),
-            pltpu.VMEM((4, GROUPS) + strip, BF16),
-            pltpu.VMEM((4, GROUPS) + strip, BF16),
+            pltpu.VMEM((GROUPS, 4) + strip, BF16),
+            pltpu.VMEM((GROUPS, 4) + strip, BF16),
             dma((2, 4)), dma((3, 2)), dma((4, 2)), dma((3,)), dma((4,)),
             dma((4, 3)), dma((4, 3)),
-            dma((GROUPS, 4, 3)), dma((GROUPS, 4, 3)), dma((4, 2)), dma((4, 2)),
+            dma((GROUPS, 4, 3)), dma((GROUPS, 4, 3)), dma((GROUPS, 4, 2)), dma((GROUPS, 4, 2)),
         ],
         compiler_params=pltpu.CompilerParams(
             collective_id=1, has_side_effects=True, vmem_limit_bytes=62 * 1024 * 1024),

time: 91.1 us -> 86.4 us (0.948)
  the two profiles are of different devices: /device:TPU:9 before, /device:TPU:25 now
where the time goes in v6:
time: 86.4 us; the launch traced here: 86.2 us
  Pallas kernels  84.3 us (98%)
  local copies, waits for them, and re-layouts  1.85 us (2%)
    pallas_call x1, Pallas kernels, migrate(): pl.pallas_call(functools.partial(migrate_kernel, factor), out_shape=jax.S...  78 us
    pallas_call x1, Pallas kernels, make_windows(): pl.pallas_call(windows_kernel, out_shape=(jax.ShapeDtypeStruct((2, N, N),...  6.32 us
    unnamed x1, local copies, waits for them, and re-layouts  1.85 us

profile of v6, /device:TPU:25, one launch (start us, length us, event | category | flops | bytes accessed | tf_op | source)
XLA Modules:
  0.0 86.2 jit_solution(4608607401071021987)
XLA Ops:
  0.0 6.3 %windows.1 = (bf16[2,512,512]{2,1,0:T(8,128)(2,1)}, f32[2,8,128]{2,1,0:T(8,128)}) custom-call(s32[1,1024,1024]{2,1,0:T(8,128)} %codes.1, f32[32]{0:T(128)} %table.3, s32[2,2]{1,0:T(2,128)} %anchors.1), custom_call_target="tpu_custom_call" | custom-call | tf_op jit(solution)/shard_map/windows/pallas_call | solution.py:119
  6.3 78.0 %migrate.1 = f32[15,16,512]{2,1,0:T(8,128)} custom-call(bf16[2,1,2,512,512]{4,3,2,1,0:T(8,128)(2,1)} %src.1, bf16[2,1,2,512,512]{4,3,2,1,0:T(8,128)(2,1)} %rec.1, bf16[2,512,512]{2,1,0:T(8,128)(2,1)} %get-tuple-element.7.win, f32[2,8,128]{2,1,0:T(8,128)} %get-tuple-element.8.means, f32[32]{0:T(128)} %table.3, bf16[4,256,256]{2,1,0:T(8,128)(2,1)} %constant.4.clone.right_ref, ...), custom_call_target="tpu_custom_call" | custom-call | tf_op jit(solution)/shard_map/migrate/pallas_call | solution.py:531
  84.3 1.9 %copy.9 = f32[1,15,16,512]{3,2,1,0:T(8,128)} copy(f32[1,15,16,512]{3,2,1,0:T(8,128)} %bitcast.1) | data formatting | bytes 983040

commit v7 on v6

--- a/solution.py
+++ b/solution.py
@@ -83,56 +83,9 @@
         mode=lax.GatherScatterMode.PROMISE_IN_BOUNDS)
 
 
-def windows_kernel(codes, table, anchors, out, means, raw, sem):
-    def fetch(s, h):
-        ox = pl.multiple_of(anchors[s, 0], N)
-        oy = pl.multiple_of(anchors[s, 1], N)
-        return pltpu.make_async_copy(
-            codes.at[0, pl.ds(ox + h * 256, 256), pl.ds(oy, N)], raw.at[s, h], sem.at[s, h])
-
-    for s in range(2):
-        for h in range(2):
-            fetch(s, h).start()
-    levels = level_row(table)
-    for s in range(2):
-        total = jnp.zeros((8, B), F32)
-        for h in range(2):
-            fetch(s, h).wait()
-
-            def rows_of(n, total):
-                take = pl.ds(pl.multiple_of(n * 32, 32), 32)
-                for q in range(4):
-                    index = raw[s, h, take, q * B:(q + 1) * B]
-                    out[s, pl.ds(pl.multiple_of(h * 256 + n * 32, 32), 32), q * B:(q + 1) * B] = (
-                        index.astype(F32).astype(BF16))
-                    got = lookup(levels, index)
-                    total = total + (got[0:8] + got[8:16]) + (got[16:24] + got[24:32])
-                return total
-
-            total = lax.fori_loop(0, 8, rows_of, total)
-        means[s] = jnp.full((8, B), jnp.sum(total) * (1.0 / (N * N)), F32)
-
-
-def make_windows(codes, table, anchors):
-    vmem = pl.BlockSpec(memory_space=pltpu.VMEM)
-    smem = pl.BlockSpec(memory_space=pltpu.SMEM)
-    return pl.pallas_call(
-        windows_kernel,
-        out_shape=(
-            jax.ShapeDtypeStruct((2, N, N), BF16),
-            jax.ShapeDtypeStruct((2, 8, B), F32),
-        ),
-        in_specs=[pl.BlockSpec(memory_space=pl.ANY), smem, smem],
-        out_specs=(vmem, vmem),
-        scratch_shapes=[pltpu.VMEM((2, 2, 256, N), jnp.int32), pltpu.SemaphoreType.DMA((2, 2))],
-        compiler_params=pltpu.CompilerParams(vmem_limit_bytes=60 * 1024 * 1024),
-        name="windows",
-    )(codes, table, anchors)
-
-
 def migrate_kernel(
-    factor, src, rec, win, means, table, right_ref, left_ref, out,
-    u, a, cbuf, mbuf, ph, sc, raw, pad, buf, r1, r2, r3, fa, fb,
+    factor, src, rec, model, table, anchors, right_ref, left_ref, out,
+    rawc, win, means, wsem, u, a, cbuf, mbuf, ph, sc, raw, pad, buf, r1, r2, r3, fa, fb,
     tsem, csend, crecv, msend, mrecv, esend, erecv, ssem, rsem, fsend, frecv,
 ):
     depth = lax.axis_index("depth")
@@ -160,6 +113,13 @@
     mine = bits(x, z)
     side = mine
 
+    loads = []
+    for qx in range(2):
+        for qy in range(2):
+            loads.append(pltpu.make_async_copy(
+                model.at[0, pl.ds(qx * N, N), pl.ds(qy * N, N)], rawc.at[qx, qy], wsem.at[qx, qy]))
+    for copy_in in loads:
+        copy_in.start()
     tops = []
     for kind, top in enumerate((src, rec)):
         for q in range(4):
@@ -171,11 +131,6 @@
     def half_rows(way):
         return pl.ds(way * (N // 2), N // 2)
 
-    for way in range(2):
-        pltpu.make_async_copy(
-            win.at[core, half_rows(way)], cbuf.at[depth, half_rows(way)], crecv.at[depth, way]).start()
-    mbuf[depth] = means[core]
-
     barrier = pltpu.get_barrier_semaphore()
     peers = [sibling, (depth, far)] + beside[0] + beside[1]
     for i in range(4):
@@ -186,6 +141,25 @@
     position = freq.astype(F32)
     angular = math.pi * (0.45 + 0.5 * (position + 0.5) / 32.0)
     levels = level_row(table)
+
+    for copy_in in loads:
+        copy_in.wait()
+    for s in range(2):
+        qx = anchors[s, 0] // N
+        qy = anchors[s, 1] // N
+
+        def rows_of(n, total):
+            take = pl.ds(pl.multiple_of(n * 32, 32), 32)
+            for q in range(4):
+                index = rawc[qx, qy, take, q * B:(q + 1) * B]
+                win[s, take, q * B:(q + 1) * B] = index.astype(F32).astype(BF16)
+                got = lookup(levels, index)
+                total = total + (got[0:8] + got[8:16]) + (got[16:24] + got[24:32])
+            return total
+
+        total = lax.fori_loop(0, N // 32, rows_of, jnp.zeros((8, B), F32))
+        means[s] = jnp.full((8, B), jnp.sum(total) * (1.0 / (N * N)), F32)
+
     pl.semaphore_wait(barrier, len(peers))
 
     def codes_to(n, way, who):
@@ -206,6 +180,11 @@
         for s in range(2):
             for way in range(2):
                 act(codes_to(s, way, beside[way][s]))
+
+    for way in range(2):
+        pltpu.make_async_copy(
+            win.at[core, half_rows(way)], cbuf.at[depth, half_rows(way)], crecv.at[depth, way]).start()
+    mbuf[depth] = means[core]
 
     mean_to(2, sibling).start()
 
@@ -252,6 +231,35 @@
         z = plane
         new = jnp.where(z < first_plane, 2, z - first_plane)
         old = jnp.where(z <= first_plane, 2, z - 1 - first_plane)
+
+        @pl.when(z != depth)
+        def _():
+            pltpu.make_async_copy(means.at[0], mbuf.at[z], mrecv.at[z]).wait()
+
+        base = mbuf[z, 0:1, :]
+        turn = angular * base
+        turn_sq = turn * turn
+        angle = angular * (levels - base)
+        squared = angle * angle
+        cos_levels = horner(COS_Q, squared)
+        sin_levels = angle * horner(SIN_Q, squared)
+
+        def operators(n):
+            rows = n * 96
+            k = rows + lax.broadcasted_iota(jnp.int32, (96, B), 0)
+            kx = (k % B) * 4 + k // B
+            kx = jnp.where(kx < N // 2, kx, kx - N).astype(F32) * (2.0 * math.pi / N)
+            left_q = turn_sq - kx * kx
+            for ry in range(3):
+                ky = lax.broadcasted_iota(jnp.int32, (1, B), 1) * 4 + ry
+                ky = jnp.where(ky < N // 2, ky, ky - N).astype(F32) * (2.0 * math.pi / N)
+                q = left_q - ky * ky
+                size = jnp.maximum(jnp.abs(q), 1e-30)
+                root = size * lax.rsqrt(size)
+                travels = q >= 0.0
+                put = slice(rows, rows + 96)
+                ph[0, ry, put, :] = jnp.where(travels, horner(COS_Q, q), jnp.exp(-root)).astype(BF16)
+                ph[1, ry, put, :] = jnp.where(travels, root * horner(SIN_Q, q), 0.0).astype(BF16)
 
         def wide(ref, kind, p, half, block):
             rows = slice(block * B, (block + 1) * B)
@@ -278,52 +286,13 @@
                 put_wide(a, kind, 1, half, r, got[B:])
             return carry
 
-        lax.fori_loop(0, 4, forward_x, 0, unroll=4)
+        for n in range(4):
+            forward_x(n, 0)
+            operators(n)
 
         @pl.when(z == first_plane + 1)
         def _():
             hand_plane(0)
-
-        for way in range(2):
-            pltpu.make_async_copy(
-                win.at[0, half_rows(way)], cbuf.at[z, half_rows(way)], crecv.at[z, way]).wait()
-
-        @pl.when(z != depth)
-        def _():
-            pltpu.make_async_copy(means.at[0], mbuf.at[z], mrecv.at[z]).wait()
-
-        base = mbuf[z, 0:1, :]
-        turn = angular * base
-        turn_sq = turn * turn
-        angle = angular * (levels - base)
-        squared = angle * angle
-        cos_levels = horner(COS_Q, squared)
-        sin_levels = angle * horner(SIN_Q, squared)
-
-        def operators(n, carry):
-            rows = n * 48
-            k = rows + lax.broadcasted_iota(jnp.int32, (48, B), 0)
-            kx = (k % B) * 4 + k // B
-            kx = jnp.where(kx < N // 2, kx, kx - N).astype(F32) * (2.0 * math.pi / N)
-            left_q = turn_sq - kx * kx
-            for ry in range(3):
-                ky = lax.broadcasted_iota(jnp.int32, (1, B), 1) * 4 + ry
-                ky = jnp.where(ky < N // 2, ky, ky - N).astype(F32) * (2.0 * math.pi / N)
-                q = left_q - ky * ky
-                size = jnp.maximum(jnp.abs(q), 1e-30)
-                root = size * lax.rsqrt(size)
-                travels = q >= 0.0
-                put = pl.ds(pl.multiple_of(rows, 16), 48)
-                ph[0, ry, put, :] = jnp.where(travels, horner(COS_Q, q), jnp.exp(-root)).astype(BF16)
-                ph[1, ry, put, :] = jnp.where(travels, root * horner(SIN_Q, q), 0.0).astype(BF16)
-            take = pl.ds(pl.multiple_of(n * 64, 64), 64)
-            for q in range(4):
-                index = cbuf[z, take, q * B:(q + 1) * B].astype(jnp.int32)
-                sc[0, q, take, :] = lookup(cos_levels, index).astype(BF16)
-                sc[1, q, take, :] = lookup(sin_levels, index).astype(BF16)
-            return carry
-
-        lax.fori_loop(0, 8, operators, 0)
 
         def along_y(rx, carry):
             prow = pl.ds(pl.multiple_of(jnp.where(rx == 3, 1, rx) * B, B), B)
@@ -356,33 +325,41 @@
 
         lax.fori_loop(0, 4, along_y, 0, unroll=4)
 
+        for way in range(2):
+            pltpu.make_async_copy(
+                win.at[0, half_rows(way)], cbuf.at[z, half_rows(way)], crecv.at[z, way]).wait()
+
         @pl.when(jnp.logical_and(z == 0, jnp.logical_and(section == 0, core == 1)))
         def _():
             section_codes(lambda c: c.start())
 
-        def inverse_x(n, carry):
-            kind, half = n % 2, n // 2
-            sign = (1 - 2 * kind).astype(F32).astype(BF16)
-            tre, tim = [], []
-            for r in range(4):
-                data = jnp.concatenate([wide(a, kind, 0, half, r), wide(a, kind, 1, half, r)], axis=0)
-                got = jnp.dot(right_ref[r], data, preferred_element_type=F32).astype(BF16)
-                tre.append(got[:B])
-                tim.append(got[B:])
-            xre, xim = join4(tre, tim)
+        for half in range(2):
             for q in range(4):
                 rows = slice(q * B, (q + 1) * B)
                 for part in range(2):
-                    cols = slice(part * B, (part + 1) * B)
-                    cre = sc[0, half * 2 + part, rows, :]
-                    cim = sc[1, half * 2 + part, rows, :] * sign
-                    gre, gim = xre[q][:, cols], xim[q][:, cols]
-                    u[new, kind, 0, half * 2 + part, rows, :] = gre * cre - gim * cim
-                    u[new, kind, 1, half * 2 + part, rows, :] = gre * cim + gim * cre
-            return carry
-
-        lax.fori_loop(0, 4, inverse_x, 0, unroll=4)
-
+                    block = half * 2 + part
+                    index = cbuf[z, rows, block * B:(block + 1) * B].astype(jnp.int32)
+                    sc[0, block, rows, :] = lookup(cos_levels, index).astype(BF16)
+                    sc[1, block, rows, :] = lookup(sin_levels, index).astype(BF16)
+            for kind in range(2):
+                tre, tim = [], []
+                for r in range(4):
+                    data = jnp.concatenate([wide(a, kind, 0, half, r), wide(a, kind, 1, half, r)], axis=0)
+                    got = jnp.dot(right_ref[r], data, preferred_element_type=F32).astype(BF16)
+                    tre.append(got[:B])
+                    tim.append(got[B:])
+                xre, xim = join4(tre, tim)
+                for q in range(4):
+                    rows = slice(q * B, (q + 1) * B)
+                    for part in range(2):
+                        block = half * 2 + part
+                        cols = slice(part * B, (part + 1) * B)
+                        cre, cim = sc[0, block, rows, :], sc[1, block, rows, :]
+                        gre, gim = xre[q][:, cols], xim[q][:, cols]
+                        rr, ii, ri, ir = gre * cre, gim * cim, gre * cim, gim * cre
+                        nre, nim = (rr - ii, ri + ir) if kind == 0 else (rr + ii, ir - ri)
+                        u[new, kind, 0, block, rows, :] = nre
+                        u[new, kind, 1, block, rows, :] = nim
         return carry
 
     lax.fori_loop(0, steps, step, 0)
@@ -523,17 +500,22 @@
             mean_to(s, beside[0][s]).wait_send()
 
 
-def migrate(src, rec, win, means, table, right, left, factor):
+def migrate(src, rec, model, table, anchors, right, left, factor):
     vmem = pl.BlockSpec(memory_space=pltpu.VMEM)
     hbm = pl.BlockSpec(memory_space=pl.ANY)
+    smem = pl.BlockSpec(memory_space=pltpu.SMEM)
     dma = pltpu.SemaphoreType.DMA
     strip = (PER, 16, B)
     return pl.pallas_call(
         functools.partial(migrate_kernel, factor),
         out_shape=jax.ShapeDtypeStruct((LAGS, 16, N), F32),
-        in_specs=[hbm, hbm, hbm, vmem, pl.BlockSpec(memory_space=pltpu.SMEM), vmem, vmem],
+        in_specs=[hbm, hbm, hbm, smem, smem, vmem, vmem],
         out_specs=vmem,
         scratch_shapes=[
+            pltpu.VMEM((2, 2, N, N), jnp.int32),
+            pltpu.VMEM((2, N, N), BF16),
+            pltpu.VMEM((2, 8, B), F32),
+            dma((2, 2)),
             pltpu.VMEM((3, 2, 2, 4, N, B), BF16),
             pltpu.VMEM((2, 2, 4, N, B), BF16),
             pltpu.VMEM((4, N, N), BF16),
@@ -555,16 +537,15 @@
         compiler_params=pltpu.CompilerParams(
             collective_id=1, has_side_effects=True, vmem_limit_bytes=62 * 1024 * 1024),
         name="migrate",
-    )(src, rec, win, means, table, right, left)
+    )(src, rec, model, table, anchors, right, left)
 
 
 def shards(source_top, receiver_top, slowness_codes, slowness_table, anchors):
     right, left = butterfly_matrices()
     right = jnp.asarray(right, BF16)
     left = jnp.asarray(left, BF16)
-    windows, means = make_windows(slowness_codes, slowness_table, anchors)
     image = migrate(
-        source_top, receiver_top, windows, means, slowness_table, right, left, 1.0 / math.sqrt(128.0))
+        source_top, receiver_top, slowness_codes, slowness_table, anchors, right, left, 1.0 / math.sqrt(128.0))
     return image[None]
 
 

time: 86.4 us -> 79.2 us (0.917)
  the two profiles are of different devices: /device:TPU:25 before, /device:TPU:8 now
where the time goes in v7:
time: 79.2 us; the launch traced here: 78.3 us
  Pallas kernels  76.5 us (97%)
  local copies, waits for them, and re-layouts  1.85 us (2%)
    pallas_call x1, Pallas kernels, migrate(): pl.pallas_call(functools.partial(migrate_kernel, factor), out_shape=jax.S...  76.5 us
    unnamed x1, local copies, waits for them, and re-layouts  1.85 us

profile of v7, /device:TPU:8, one launch (start us, length us, event | category | flops | bytes accessed | tf_op | source)
XLA Modules:
  0.0 78.3 jit_solution(15535324198399367548)
XLA Ops:
  0.0 76.5 %migrate.1 = f32[15,16,512]{2,1,0:T(8,128)} custom-call(bf16[2,1,2,512,512]{4,3,2,1,0:T(8,128)(2,1)} %src.1, bf16[2,1,2,512,512]{4,3,2,1,0:T(8,128)(2,1)} %rec.1, s32[1,1024,1024]{2,1,0:T(8,128)} %model.1, f32[32]{0:T(128)} %table.1, s32[2,2]{1,0:T(2,128)} %anchors.1, bf16[4,256,256]{2,1,0:T(8,128)(2,1)} %constant.4.clone.right_ref, ...), custom_call_target="tpu_custom_call" | custom-call | tf_op jit(solution)/shard_map/migrate/pallas_call | solution.py:509
  76.5 1.9 %copy.9 = f32[1,15,16,512]{3,2,1,0:T(8,128)} copy(f32[1,15,16,512]{3,2,1,0:T(8,128)} %bitcast.1) | data formatting | bytes 983040

commit v8 on v7

--- a/solution.py
+++ b/solution.py
@@ -111,7 +111,14 @@
         return [((ix + 1) // 2) % 2, ix // 2, ((iz + 1) // 2) % 2, iz // 2]
 
     mine = bits(x, z)
-    side = mine
+    at_home = [mine[i] == yh for i in range(4)]
+    first = x + core * (z - x)
+    second = z + core * (x - z)
+    near = [ring[d] + core * (ring[(d + 2) % 4] - ring[d]) for d in range(4)]
+    far_near = [r - 16 * yh + 16 * (1 - yh) for r in near]
+    own = bits(first, second)
+    first_stride = 16 + 48 * core
+    second_stride = 64 - 48 * core
 
     loads = []
     for qx in range(2):
@@ -132,9 +139,9 @@
         return pl.ds(way * (N // 2), N // 2)
 
     barrier = pltpu.get_barrier_semaphore()
-    peers = [sibling, (depth, far)] + beside[0] + beside[1]
+    peers = [sibling, (depth, far), (other, far)] + beside[0] + beside[1]
     for i in range(4):
-        peers += [(depth, ring[i]), (other, ring[i]), (depth, far_ring[i])]
+        peers += [(depth, ring[i]), (other, ring[i]), (depth, far_ring[i]), (other, far_ring[i])]
     for who in peers:
         pl.semaphore_signal(barrier, inc=1, device_id=who, device_id_type=MESH)
 
@@ -203,26 +210,19 @@
     def window(i, half):
         return pl.ds(pl.multiple_of(half * 240, 16), 272)
 
-    def hand(i, n):
-        plane = (1 - core, core, 1 - core)[n]
-        half = (side[i], 1 - side[i], 1 - side[i])[n]
-        who = (sibling, (depth, ring[i]), (other, ring[i]))[n]
+    def hand(q, j, n):
+        part = (2 * (1 - core) + j, 2 * core + j, 2 * (1 - core) + j)[n]
+        half = (own[2 + j], 1 - own[j], 1 - own[2 + j])[n]
+        who = (sibling, (depth, near[j]), (other, near[2 + j]))[n]
         return pltpu.make_async_remote_copy(
-            src_ref=u.at[plane, :, :, i, window(i, half)], dst_ref=raw.at[i, n],
-            send_sem=esend.at[i, n], recv_sem=erecv.at[i, n],
+            src_ref=u.at[q, :, :, part, window(part, half)], dst_ref=raw.at[q, j, n],
+            send_sem=esend.at[q, j, n], recv_sem=erecv.at[q, j, n],
             device_id=who, device_id_type=MESH)
 
     def hand_plane(q):
-        @pl.when(core == q)
-        def _():
-            for i in range(4):
-                hand(i, 1).start()
-
-        @pl.when(core != q)
-        def _():
-            for n in (2, 0):
-                for i in range(4):
-                    hand(i, n).start()
+        for n in (2, 1, 0):
+            for j in range(2):
+                hand(q, j, n).start()
 
     for copy_in in tops:
         copy_in.wait()
@@ -364,131 +364,147 @@
 
     lax.fori_loop(0, steps, step, 0)
 
-    for i in range(4):
-        for s in range(4):
+    for q in range(2):
+        for j in range(2):
+            for s in range(4):
+                for k in range(2):
+                    for p in range(2):
+                        pad[q, j, s, k, p, 0:8, :] = jnp.zeros((8, B), F32)
+                        pad[q, j, s, k, p, 280:288, :] = jnp.zeros((8, B), F32)
+    hand_plane(1)
+
+    def gather_plane(q):
+        for j in range(2):
             for k in range(2):
                 for p in range(2):
-                    pad[i, s, k, p, 0:8, :] = jnp.zeros((8, B), F32)
-                    pad[i, s, k, p, 280:288, :] = jnp.zeros((8, B), F32)
-    hand_plane(1)
-
-    for i in range(4):
-        for k in range(2):
-            for p in range(2):
-                pad[i, 0, k, p, 8:280, :] = u[core, k, p, i, window(i, side[i]), :].astype(F32)
-    for n in range(3):
-        for i in range(4):
-            hand(i, n).wait_recv()
-            for k in range(2):
-                for p in range(2):
-                    pad[i, n + 1, k, p, 8:280, :] = raw[i, n, k, p].astype(F32)
-
-    def weight(d, i):
-        return (1, 8, 4, 2)[(d - i) % 4]
-
-    flip_x = [[(mine[d] + bits(v, 0)[d]) % 2 for d in range(2)] for v in range(4)]
-    slot_x = [[sum(flip_x[v][d] * weight(d, i) for d in range(2)) for i in range(4)] for v in range(4)]
-    shift = [side[i] * 16 for i in range(4)]
-
-    def produce(g):
+                    pad[q, j, 0, k, p, 8:280, :] = u[q, k, p, 2 * core + j, window(j, own[j]), :].astype(F32)
+        for n in range(3):
+            for j in range(2):
+                hand(q, j, n).wait_recv()
+                for k in range(2):
+                    for p in range(2):
+                        pad[q, j, n + 1, k, p, 8:280, :] = raw[q, j, n, k, p].astype(F32)
+
+    def weight(d, j):
+        return (1, 8, 4, 2)[(d - j) % 4]
+
+    flip_1 = [[(own[d] + bits(v, 0)[d]) % 2 for d in range(2)] for v in range(4)]
+    slot_1 = [[sum(flip_1[v][d] * weight(d, j) for d in range(2)) for j in range(2)] for v in range(4)]
+
+    def produce(q, g):
         def body(n, carry):
             theirs = bits(0, n)
-            flip_z = [(mine[d] + theirs[d]) % 2 for d in (2, 3)]
-            slot_z = [sum(flip_z[d - 2] * weight(d, i) for d in (2, 3)) for i in range(4)]
+            flip_2 = [(own[d] + theirs[d]) % 2 for d in (2, 3)]
+            slot_2 = [sum(flip_2[d - 2] * weight(d, j) for d in (2, 3)) for j in range(2)]
             for v in range(4):
-                for i in range(4):
-                    row = pl.multiple_of(n * 64 + v * 16 + shift[i], 16)
-                    slot = slot_z[i] + slot_x[v][i]
+                for j in range(2):
+                    row = pl.multiple_of(n * second_stride + v * first_stride + own[j] * 16, 16)
+                    slot = slot_2[j] + slot_1[v][j]
                     for l in range(PER):
                         h = g * PER + l - LAG
                         total = None
                         for s in range(4):
                             for p in range(2):
-                                left = pad[i, s, 0, p, pl.ds(row + (8 - h), 16), :]
-                                right = pad[i, s, 1, p, pl.ds(row + (8 + h), 16), :]
+                                left = pad[q, j, s, 0, p, pl.ds(row + (8 - h), 16), :]
+                                right = pad[q, j, s, 1, p, pl.ds(row + (8 + h), 16), :]
                                 term = left * right
                                 total = term if total is None else total + term
-                        buf[g, i, slot, l] = total.astype(BF16)
+                        buf[q, g, j, slot, l] = total.astype(BF16)
             return carry
         lax.fori_loop(0, 4, body, 0)
 
     recv = (None, r1, r2, r3)
 
-    def copy(g, i, t):
+    def copy(q, g, j, t):
         half = 16 >> t
         return pltpu.make_async_remote_copy(
-            src_ref=buf.at[g, i, pl.ds(half, half)], dst_ref=recv[t].at[g, i],
-            send_sem=ssem.at[g, i, t - 1], recv_sem=rsem.at[g, i, t - 1],
-            device_id=(depth, ring[(i + t) % 4]), device_id_type=MESH)
-
-    def last(g, i, slot, who, place):
+            src_ref=buf.at[q, g, j, pl.ds(half, half)], dst_ref=recv[t].at[q, g, j],
+            send_sem=ssem.at[q, g, j, t - 1], recv_sem=rsem.at[q, g, j, t - 1],
+            device_id=(depth, near[(j + t) % 4]), device_id_type=MESH)
+
+    def last(q, g, j, slot, who, place):
+        part = 2 * core + j
         return pltpu.make_async_remote_copy(
-            src_ref=buf.at[g, i, slot], dst_ref=(fa, fb)[place].at[g, i],
-            send_sem=fsend.at[g, i, slot], recv_sem=frecv.at[g, i, place],
+            src_ref=buf.at[q, g, j, slot], dst_ref=(fa, fb)[place].at[g, part],
+            send_sem=fsend.at[q, g, j, slot], recv_sem=frecv.at[g, part, place],
             device_id=who, device_id_type=MESH)
 
-    at_home = [side[i] == yh for i in range(4)]
-
-    def sends_last(g, i, act):
-        @pl.when(at_home[i])
-        def _():
-            act(last(g, i, 1, (depth, ring[i]), 0))
-
-        @pl.when(jnp.logical_not(at_home[i]))
-        def _():
-            act(last(g, i, 0, (depth, far), 0))
-            act(last(g, i, 1, (depth, far_ring[i]), 1))
-
-    def arrive(g, i, t):
-        copy(g, i, t).wait_recv()
+    def sends_last(q, g, j, act):
+        owner = first_plane + q
+
+        @pl.when(own[j] == yh)
+        def _():
+            act(last(q, g, j, 1, (owner, near[j]), 0))
+
+        @pl.when(jnp.logical_and(own[j] == yh, core != q))
+        def _():
+            act(last(q, g, j, 0, sibling, 1))
+
+        @pl.when(own[j] != yh)
+        def _():
+            act(last(q, g, j, 0, (owner, far), 0))
+            act(last(q, g, j, 1, (owner, far_near[j]), 1))
+
+    def arrive(q, g, j, t):
+        copy(q, g, j, t).wait_recv()
         half = 16 >> t
 
         def body(n, carry):
             for k in (half - 1 - 2 * n, half - 2 - 2 * n):
-                buf[g, i, k] = buf[g, i, k] + recv[t][g, i, k]
+                buf[q, g, j, k] = buf[q, g, j, k] + recv[t][q, g, j, k]
             return carry
         lax.fori_loop(0, half // 2, body, 0)
         if t < 3:
-            copy(g, i, t + 1).start()
+            copy(q, g, j, t + 1).start()
         else:
-            sends_last(g, i, lambda c: c.start())
+            sends_last(q, g, j, lambda c: c.start())
+
+    def came(g, i, place):
+        pltpu.make_async_remote_copy(
+            src_ref=buf.at[0, g, 0, 0], dst_ref=(fa, fb)[place].at[g, i],
+            send_sem=fsend.at[0, g, 0, 0], recv_sem=frecv.at[g, i, place],
+            device_id=sibling, device_id_type=MESH).wait_recv()
 
     def finish(g, i):
-        last(g, i, 0, (depth, far), 0).wait_recv()
+        came(g, i, 0)
         put = (slice(g * PER, (g + 1) * PER), slice(None), slice(i * B, (i + 1) * B))
-
-        @pl.when(at_home[i])
-        def _():
-            out[put] = (buf[g, i, 0].astype(F32) + fa[g, i].astype(F32)) * factor
-
-        @pl.when(jnp.logical_not(at_home[i]))
-        def _():
-            last(g, i, 1, (depth, far_ring[i]), 1).wait_recv()
+        kept = jnp.logical_and(at_home[i], core == i // 2)
+
+        @pl.when(kept)
+        def _():
+            out[put] = (buf[core, g, i % 2, 0].astype(F32) + fa[g, i].astype(F32)) * factor
+
+        @pl.when(jnp.logical_not(kept))
+        def _():
+            came(g, i, 1)
             out[put] = (fa[g, i].astype(F32) + fb[g, i].astype(F32)) * factor
 
-    for g in range(GROUPS):
-        produce(g)
-        for i in range(4):
-            copy(g, i, 1).start()
+    events = [(q, g) for q in range(2) for g in range(GROUPS)]
+    for e, (q, g) in enumerate(events):
+        if g == 0:
+            gather_plane(q)
+        produce(q, g)
+        for j in range(2):
+            copy(q, g, j, 1).start()
         for t in (3, 2, 1):
-            if g - 1 - t >= 0:
-                for i in range(4):
-                    arrive(g - 1 - t, i, t)
-    left = [(g, t) for t in (1, 2, 3) for g in range(GROUPS) if g + t > GROUPS - 2]
-    for g, t in sorted(left, key=lambda gt: (gt[0] + gt[1], gt[1])):
-        for i in range(4):
-            arrive(g, i, t)
+            if e - 1 - t >= 0:
+                for j in range(2):
+                    arrive(*events[e - 1 - t], j, t)
+    still = [(e, t) for t in (1, 2, 3) for e in range(len(events)) if e + t > len(events) - 2]
+    for e, t in sorted(still, key=lambda et: (et[0] + et[1], et[1])):
+        for j in range(2):
+            arrive(*events[e], j, t)
     for g in range(GROUPS):
         for i in range(4):
             finish(g, i)
-    for i in range(4):
-        for n in range(3):
-            hand(i, n).wait_send()
-    for g in range(GROUPS):
-        for i in range(4):
-            for t in (1, 2, 3):
-                copy(g, i, t).wait_send()
-            sends_last(g, i, lambda c: c.wait_send())
+    for q in range(2):
+        for j in range(2):
+            for n in range(3):
+                hand(q, j, n).wait_send()
+            for g in range(GROUPS):
+                for t in (1, 2, 3):
+                    copy(q, g, j, t).wait_send()
+                sends_last(q, g, j, lambda c: c.wait_send())
     for way in range(2):
         codes_to(2, way, sibling).wait_send()
     mean_to(2, sibling).wait_send()
@@ -522,17 +538,17 @@
             pltpu.VMEM((4, 8, B), F32),
             pltpu.VMEM((2, 3, 3 * B, B), BF16),
             pltpu.VMEM((2, 4, N, B), BF16),
-            pltpu.VMEM((4, 3, 2, 2, 272, B), BF16),
-            pltpu.VMEM((4, 4, 2, 2, 288, B), F32),
-            pltpu.VMEM((GROUPS, 4, 16) + strip, BF16),
-            pltpu.VMEM((GROUPS, 4, 8) + strip, BF16),
-            pltpu.VMEM((GROUPS, 4, 4) + strip, BF16),
-            pltpu.VMEM((GROUPS, 4, 2) + strip, BF16),
+            pltpu.VMEM((2, 2, 3, 2, 2, 272, B), BF16),
+            pltpu.VMEM((2, 2, 4, 2, 2, 288, B), F32),
+            pltpu.VMEM((2, GROUPS, 2, 16) + strip, BF16),
+            pltpu.VMEM((2, GROUPS, 2, 8) + strip, BF16),
+            pltpu.VMEM((2, GROUPS, 2, 4) + strip, BF16),
+            pltpu.VMEM((2, GROUPS, 2, 2) + strip, BF16),
             pltpu.VMEM((GROUPS, 4) + strip, BF16),
             pltpu.VMEM((GROUPS, 4) + strip, BF16),
             dma((2, 4)), dma((3, 2)), dma((4, 2)), dma((3,)), dma((4,)),
-            dma((4, 3)), dma((4, 3)),
-            dma((GROUPS, 4, 3)), dma((GROUPS, 4, 3)), dma((GROUPS, 4, 2)), dma((GROUPS, 4, 2)),
+            dma((2, 2, 3)), dma((2, 2, 3)),
+            dma((2, GROUPS, 2, 3)), dma((2, GROUPS, 2, 3)), dma((2, GROUPS, 2, 2)), dma((GROUPS, 4, 2)),
         ],
         compiler_params=pltpu.CompilerParams(
             collective_id=1, has_side_effects=True, vmem_limit_bytes=62 * 1024 * 1024),

time: 79.2 us -> 94 us (1.19)
  the two profiles are of different devices: /device:TPU:8 before, /device:TPU:27 now
where the time goes in v8:
time: 94 us; the launch traced here: 93.8 us
  Pallas kernels  91.9 us (98%)
  local copies, waits for them, and re-layouts  1.85 us (2%)
    pallas_call x1, Pallas kernels, migrate(): pl.pallas_call(functools.partial(migrate_kernel, factor), out_shape=jax.S...  91.9 us

profile of v8, /device:TPU:27, one launch (start us, length us, event | category | flops | bytes accessed | tf_op | source)
XLA Modules:
  0.0 93.8 jit_solution(10227893775640279121)
XLA Ops:
  0.0 91.9 %migrate.1 = f32[15,16,512]{2,1,0:T(8,128)} custom-call(bf16[2,1,2,512,512]{4,3,2,1,0:T(8,128)(2,1)} %src.1, bf16[2,1,2,512,512]{4,3,2,1,0:T(8,128)(2,1)} %rec.1, s32[1,1024,1024]{2,1,0:T(8,128)} %model.1, f32[32]{0:T(128)} %table.1, s32[2,2]{1,0:T(2,128)} %anchors.1, bf16[4,256,256]{2,1,0:T(8,128)(2,1)} %constant.4.clone.right_ref, ...), custom_call_target="tpu_custom_call" | custom-call | tf_op jit(solution)/shard_map/migrate/pallas_call | solution.py:525
  91.9 1.9 %copy.9 = f32[1,15,16,512]{3,2,1,0:T(8,128)} copy(f32[1,15,16,512]{3,2,1,0:T(8,128)} %bitcast.1) | data formatting | bytes 983040

commit v9 on v8

--- a/solution.py
+++ b/solution.py
@@ -13,7 +13,7 @@
 LAGS = 2 * LAG + 1
 N = 512
 B = 128
-GROUPS = 5
+GROUPS = 3
 PER = LAGS // GROUPS
 MESH = pl.DeviceIdType.MESH
 F32 = jnp.float32
@@ -486,14 +486,10 @@
         produce(q, g)
         for j in range(2):
             copy(q, g, j, 1).start()
-        for t in (3, 2, 1):
-            if e - 1 - t >= 0:
-                for j in range(2):
-                    arrive(*events[e - 1 - t], j, t)
-    still = [(e, t) for t in (1, 2, 3) for e in range(len(events)) if e + t > len(events) - 2]
-    for e, t in sorted(still, key=lambda et: (et[0] + et[1], et[1])):
-        for j in range(2):
-            arrive(*events[e], j, t)
+    for t in (1, 2, 3):
+        for event in events:
+            for j in range(2):
+                arrive(*event, j, t)
     for g in range(GROUPS):
         for i in range(4):
             finish(g, i)

time: 94 us -> 77.2 us (0.82)
  the two profiles are of different devices: /device:TPU:27 before, /device:TPU:25 now
where the time goes in v9:
time: 77.2 us; the launch traced here: 77 us
  Pallas kernels  75.2 us (97%)
  local copies, waits for them, and re-layouts  1.85 us (2%)
    pallas_call x1, Pallas kernels, migrate(): pl.pallas_call(functools.partial(migrate_kernel, factor), out_shape=jax.S...  75.2 us
    unnamed x1, local copies, waits for them, and re-layouts  1.85 us

profile of v9, /device:TPU:25, one launch (start us, length us, event | category | flops | bytes accessed | tf_op | source)
XLA Modules:
  0.0 77.0 jit_solution(4274180397610331298)
XLA Ops:
  0.0 75.2 %migrate.1 = f32[15,16,512]{2,1,0:T(8,128)} custom-call(bf16[2,1,2,512,512]{4,3,2,1,0:T(8,128)(2,1)} %src.1, bf16[2,1,2,512,512]{4,3,2,1,0:T(8,128)(2,1)} %rec.1, s32[1,1024,1024]{2,1,0:T(8,128)} %model.1, f32[32]{0:T(128)} %table.1, s32[2,2]{1,0:T(2,128)} %anchors.1, bf16[4,256,256]{2,1,0:T(8,128)(2,1)} %constant.4.clone.right_ref, ...), custom_call_target="tpu_custom_call" | custom-call | tf_op jit(solution)/shard_map/migrate/pallas_call | solution.py:521
  75.2 1.9 %copy.9 = f32[1,15,16,512]{3,2,1,0:T(8,128)} copy(f32[1,15,16,512]{3,2,1,0:T(8,128)} %bitcast.1) | data formatting | bytes 983040

commit v10 on v9

--- a/solution.py
+++ b/solution.py
@@ -84,8 +84,8 @@
 
 
 def migrate_kernel(
-    factor, src, rec, model, table, anchors, right_ref, left_ref, out,
-    rawc, win, means, wsem, u, a, cbuf, mbuf, ph, sc, raw, pad, buf, r1, r2, r3, fa, fb,
+    factor, src, rec, model, table, anchors, right_in, left_in, out,
+    right_ref, left_ref, msem, rawc, win, means, wsem, u, a, cbuf, mbuf, ph, sc, raw, pad, buf, r1, r2, r3, fa, fb,
     tsem, csend, crecv, msend, mrecv, esend, erecv, ssem, rsem, fsend, frecv,
 ):
     depth = lax.axis_index("depth")
@@ -132,6 +132,8 @@
         for q in range(4):
             tops.append(pltpu.make_async_copy(
                 top.at[core, 0, :, :, pl.ds(q * B, B)], u.at[2, kind, :, q], tsem.at[kind, q]))
+    tops.append(pltpu.make_async_copy(left_in, left_ref, msem.at[0]))
+    tops.append(pltpu.make_async_copy(right_in, right_ref, msem.at[1]))
     for copy_in in tops:
         copy_in.start()
 
@@ -286,13 +288,13 @@
                 put_wide(a, kind, 1, half, r, got[B:])
             return carry
 
+        @pl.when(z == first_plane + 1)
+        def _():
+            hand_plane(0)
+
         for n in range(4):
             forward_x(n, 0)
             operators(n)
-
-        @pl.when(z == first_plane + 1)
-        def _():
-            hand_plane(0)
 
         def along_y(rx, carry):
             prow = pl.ds(pl.multiple_of(jnp.where(rx == 3, 1, rx) * B, B), B)
@@ -453,7 +455,7 @@
             for k in (half - 1 - 2 * n, half - 2 - 2 * n):
                 buf[q, g, j, k] = buf[q, g, j, k] + recv[t][q, g, j, k]
             return carry
-        lax.fori_loop(0, half // 2, body, 0)
+        lax.fori_loop(0, half // 2, body, 0, unroll=True)
         if t < 3:
             copy(q, g, j, t + 1).start()
         else:
@@ -514,16 +516,19 @@
 
 def migrate(src, rec, model, table, anchors, right, left, factor):
     vmem = pl.BlockSpec(memory_space=pltpu.VMEM)
-    hbm = pl.BlockSpec(memory_space=pl.ANY)
+    hbm = pl.BlockSpec(memory_space=pltpu.HBM)
     smem = pl.BlockSpec(memory_space=pltpu.SMEM)
     dma = pltpu.SemaphoreType.DMA
     strip = (PER, 16, B)
     return pl.pallas_call(
         functools.partial(migrate_kernel, factor),
         out_shape=jax.ShapeDtypeStruct((LAGS, 16, N), F32),
-        in_specs=[hbm, hbm, hbm, smem, smem, vmem, vmem],
+        in_specs=[hbm, hbm, hbm, smem, smem, hbm, hbm],
         out_specs=vmem,
         scratch_shapes=[
+            pltpu.VMEM((4, 2 * B, 2 * B), BF16),
+            pltpu.VMEM((4, 2 * B, 2 * B), BF16),
+            dma((2,)),
             pltpu.VMEM((2, 2, N, N), jnp.int32),
             pltpu.VMEM((2, N, N), BF16),
             pltpu.VMEM((2, 8, B), F32),

time: 77.2 us -> 74.9 us (0.970)
  the two profiles are of different devices: /device:TPU:25 before, /device:TPU:9 now
where the time goes in v10:
time: 74.9 us; the launch traced here: 74.7 us
  Pallas kernels  72.9 us (97%)
  local copies, waits for them, and re-layouts  1.85 us (2%)
    pallas_call x1, Pallas kernels, migrate(): pl.pallas_call(functools.partial(migrate_kernel, factor), out_shape=jax.S...  72.9 us
    unnamed x1, local copies, waits for them, and re-layouts  1.85 us

profile of v10, /device:TPU:9, one launch (start us, length us, event | category | flops | bytes accessed | tf_op | source)
XLA Modules:
  0.0 74.7 jit_solution(18116157203491337788)
XLA Ops:
  0.0 72.9 %migrate.1 = f32[15,16,512]{2,1,0:T(8,128)} custom-call(bf16[2,1,2,512,512]{4,3,2,1,0:T(8,128)(2,1)} %src.1, bf16[2,1,2,512,512]{4,3,2,1,0:T(8,128)(2,1)} %rec.1, s32[1,1024,1024]{2,1,0:T(8,128)} %model.1, f32[32]{0:T(128)} %table.1, s32[2,2]{1,0:T(2,128)} %anchors.1, bf16[4,256,256]{2,1,0:T(8,128)(2,1)} %constant.4.clone.right_in, ...), custom_call_target="tpu_custom_call" | custom-call | tf_op jit(solution)/shard_map/migrate/pallas_call | solution.py:523
  72.9 1.9 %copy.9 = f32[1,15,16,512]{3,2,1,0:T(8,128)} copy(f32[1,15,16,512]{3,2,1,0:T(8,128)} %bitcast.1) | data formatting | bytes 983040
